TPU v7x, 256 devices: a whole 4x4x8 slice. The times are simulated.
256 devices in a mesh: segment: 2 (over core), expert: 128 (over x, z, y).
Axes of the slice: x: 4, y: 4, z: 8, core: 2. Of those that a mesh axis runs over, the one named last changes fastest.
Arguments:
- latents: float32 [4, 4096, 16], P(None, 'expert'), may hold values from -6 to 6
- cond: float32 [8, 1536], replicated, may hold values from -3 to 3
- w_embed: float32 [16, 1536], replicated, may hold values from -1.5 to 1.5
- modulation: float32 [2, 8, 3, 1536], P('segment'), may hold values from -4.5 to 4.5
- router: bfloat16 [2, 1536, 16], P('segment'), may hold values from -0.15625 to 0.15625
- w_in: bfloat16 [2, 128, 1536, 768], P('segment', 'expert'), may hold values from -0.15625 to 0.15625
- w_out: bfloat16 [2, 128, 768, 1536], P('segment', 'expert'), may hold values from -0.078125 to 0.078125
- routes: int32 [2, 4, 4096, 2], P('segment', None, 'expert'), may hold values from 0 to 15, all different within a row; in each aligned block of 32 rows (0 to 31, 32 to 63, ..., all dimensions but the last counted through in order) at most 5 rows name the same one
- w_final: bfloat16 [1536, 16], replicated, may hold values from -0.15625 to 0.15625
Outputs:
- x_next: float32 [4, 4096, 16], P('segment', 'expert')
- post_mean: float32 [8, 256, 16], replicated
- post_var: float32 [8, 256, 16], replicated
Inputs may be any that keep to these rules, and one draw needn't show every extreme that they name: `routes`: in every layer and micro-batch, no expert is named by more than 5 of one device's 32 rows, a bound that some block reaches of them; a row names two different experts.
All inputs are finite; a program needn't handle non-finite values.
Results may differ from a plain program's by a relative error of at most 0.01.
Values may be sent and summed in bfloat16 or wider, within the bound.
A program may use at most 128 MiB of HBM per device.

v0:
```python
import jax
import jax.numpy as jnp
from jax import lax
from jax.sharding import PartitionSpec as P

SAMPLES = 8
SEQ = 256
CAP = 5


epsilon = 1e-06
time_step = 0.25
time_left = 0.5


def from_behind(block, axis, distance):
    devices = range(lax.axis_size(axis))
    route = [(i - distance, i) for i in devices if i - distance in devices]
    return lax.ppermute(block, axis, route)


def normalize(values_in):
    values_in = values_in.astype(jnp.float32)
    centered = values_in - jnp.mean(values_in, axis=-1, keepdims=True)
    variance = jnp.mean(centered * centered, axis=-1, keepdims=True)
    return centered * lax.rsqrt(variance + epsilon)


def position_table(positions, model_width):
    half_width = model_width // 2
    frequency = jnp.exp(-jnp.log(10000.0) * jnp.arange(half_width, dtype=jnp.float32) / half_width)
    angles = positions.astype(jnp.float32)[:, None] * frequency[None, :]
    return jnp.concatenate([jnp.sin(angles), jnp.cos(angles)], axis=-1)


def make_expert(w_first, w_second, active, received):

    def compute(rows_in):
        inner_act = jnp.einsum("skd,dh->skh", rows_in, w_first, preferred_element_type=jnp.float32)
        inner_act = jax.nn.gelu(inner_act, approximate=True).astype(jnp.bfloat16)
        return jnp.einsum(
            "skh,hd->skd", inner_act, w_second, preferred_element_type=jnp.float32
        ).astype(jnp.bfloat16)

    def skipped(rows_in):
        return jnp.zeros_like(rows_in)

    partial_value = lax.cond(active, compute, skipped, received)
    return lax.all_to_all(partial_value, "expert", split_axis=0, concat_axis=0, tiled=True)


def local(latents, cond, w_embed, modulation, router, w_in, w_out, routes, w_final):
    segment_index = lax.axis_index("segment")
    device = lax.axis_index("expert")
    devices = lax.axis_size("expert")
    micro_count, rows_dev, patch_dim = latents.shape
    experts = router.shape[2]
    model_width = cond.shape[1]
    prompt_count = cond.shape[0]
    splits = devices // experts
    capacity = CAP
    rows_all = rows_dev * devices
    per_step = 1
    slot_count = per_step * capacity
    half_count = micro_count // 2
    expert_ids = jnp.arange(experts, dtype=jnp.int32)
    slot_ids = jnp.arange(capacity, dtype=jnp.int32)
    row_ids = jnp.arange(rows_dev, dtype=jnp.int32)

    def row_anchor(micro):
        row_start = micro * rows_all + device * rows_dev
        return (row_start // (SEQ * SAMPLES), row_start % SEQ)

    map_sum = jnp.zeros((prompt_count, SEQ, patch_dim), jnp.float32)
    map_sq = jnp.zeros((prompt_count, SEQ, patch_dim), jnp.float32)
    group_count = micro_count // per_step
    step_count = group_count + 1
    incoming = jnp.zeros((per_step, rows_dev, model_width), jnp.bfloat16)
    velocity_rows = jnp.zeros((micro_count, rows_dev, patch_dim), jnp.float32)
    for step_now in range(step_count):
        group_now = step_now - segment_index
        active = jnp.logical_and(group_now >= 0, group_now < group_count)
        micro_start = jnp.clip(group_now, 0, group_count - 1) * per_step
        embed_micro = micro_start + 0
        embed_prompt, embed_pos_start = row_anchor(embed_micro)
        latent_rows = lax.dynamic_index_in_dim(latents, embed_micro, 0, keepdims=False)
        cond_row = lax.dynamic_index_in_dim(cond, embed_prompt, 0, keepdims=True)
        embedded = (
            jnp.dot(latent_rows, w_embed, precision=lax.Precision.HIGHEST)
            + position_table(embed_pos_start + row_ids, model_width)
            + cond_row
        )
        pieces = [embedded.astype(jnp.bfloat16)]
        fresh_rows = jnp.stack(pieces)
        hidden = jnp.where(segment_index == 0, fresh_rows, incoming)
        moe_prompt, moe_pos_start = row_anchor(micro_start + 0)
        mod_list = [lax.dynamic_index_in_dim(modulation[0], moe_prompt, 0, keepdims=False)]
        mod_rows = jnp.stack(mod_list)
        shift_rows = mod_rows[:, 0][:, None, :]
        scale_rows = mod_rows[:, 1][:, None, :]
        gate_rows = mod_rows[:, 2][:, None, :]
        normed = (normalize(hidden) * (1.0 + scale_rows) + shift_rows).astype(jnp.bfloat16)
        logits = jnp.einsum("grd,de->gre", normed, router[0], preferred_element_type=jnp.float32)
        chosen = lax.dynamic_slice_in_dim(routes[0], micro_start, per_step, 0)
        picked = jnp.take_along_axis(logits, chosen, axis=2)
        gate_probs = jax.nn.sigmoid(picked)
        mix_weights = gate_probs / jnp.sum(gate_probs, axis=2, keepdims=True)
        onehot = (chosen[..., None] == expert_ids).astype(jnp.int32)
        flat_hot = onehot.reshape(per_step, rows_dev * 2, experts)
        before = jnp.cumsum(flat_hot, axis=1) - flat_hot
        slot_index = jnp.sum(flat_hot * before, axis=2).reshape(per_step, rows_dev, 2)
        slot_hot = (slot_index[..., None] == slot_ids).astype(jnp.float32)
        expert_hot = onehot.astype(jnp.float32)
        spread = jnp.einsum("grke,grkc->gecr", expert_hot, slot_hot).astype(jnp.bfloat16)
        packed = jnp.einsum(
            "gecr,grd->egcd", spread, normed, preferred_element_type=jnp.float32
        ).astype(jnp.bfloat16)
        outgoing = jnp.broadcast_to(packed, (experts, splits, slot_count, model_width)).reshape(
            devices, slot_count, model_width
        )
        returned = make_expert(
            w_in[0, 0],
            w_out[0, 0],
            active,
            lax.all_to_all(outgoing, "expert", split_axis=0, concat_axis=0, tiled=True),
        )
        summed = jnp.sum(
            returned.reshape(experts, splits, slot_count, model_width).astype(jnp.float32), axis=1
        )
        summed = summed.reshape(experts, per_step, capacity, model_width)
        mixing = jnp.einsum("grke,grkc,grk->grec", expert_hot, slot_hot, mix_weights)
        moe_out = jnp.einsum("grec,egcd->grd", mixing, summed, precision=lax.Precision.HIGHEST)
        hidden = (hidden.astype(jnp.float32) + gate_rows * moe_out).astype(jnp.bfloat16)
        if step_now + 1 < step_count:
            incoming = from_behind(hidden, "segment", 1)
        final_norm = normalize(hidden).astype(jnp.bfloat16)
        velocity_rows = lax.dynamic_update_slice_in_dim(
            velocity_rows,
            jnp.einsum("grd,dp->grp", final_norm, w_final, preferred_element_type=jnp.float32),
            micro_start,
            0,
        )
    live_mask = (segment_index == 1).astype(jnp.float32)
    velocity_all = lax.psum(velocity_rows * live_mask, "segment")
    own_start = segment_index * half_count
    own_velocity = lax.dynamic_slice_in_dim(velocity_all, own_start, half_count, 0)
    own_latents = lax.dynamic_slice_in_dim(latents, own_start, half_count, 0)
    own_rows = own_latents + time_step * own_velocity
    own_clean = own_latents + time_left * own_velocity
    for member in range(half_count):
        add_map_sum = map_sum
        add_map_sq = map_sq
        prompt, pos_start = row_anchor(own_start + member)
        block_rows = own_clean[member][None]
        corner = (prompt, pos_start, jnp.int32(0))
        add_map_sum = lax.dynamic_update_slice(
            add_map_sum,
            lax.dynamic_slice(add_map_sum, corner, (1, rows_dev, patch_dim)) + block_rows,
            corner,
        )
        add_map_sq = lax.dynamic_update_slice(
            add_map_sq,
            lax.dynamic_slice(add_map_sq, corner, (1, rows_dev, patch_dim))
            + block_rows * block_rows,
            corner,
        )
        map_sum = add_map_sum
        map_sq = add_map_sq
    map_total, square_sum = lax.psum((map_sum, map_sq), ("segment", "expert"))
    mean_map = map_total / SAMPLES
    variance = square_sum / SAMPLES - mean_map * mean_map
    return (own_rows, mean_map, variance)


def solution(mesh):
    placed = (
        P(None, "expert", None),
        P(),
        P(),
        P("segment", None, None, None),
        P("segment", None, None),
        P("segment", "expert", None, None),
        P("segment", "expert", None, None),
        P("segment", None, "expert", None),
        P(),
    )
    return jax.shard_map(
        local,
        mesh=mesh,
        in_specs=placed,
        out_specs=(P("segment", "expert", None), P(), P()),
        check_vma=False,
    )
```

profile of v0, /device:TPU:1, one launch (start us, length us, event | category | flops | bytes accessed | tf_op | source)
XLA Modules:
  0.0 1189.4 jit_solution(656601369311487716)
XLA Ops:
  18.7 16.3 %all-to-all-start = ((bf16[128,5,1536]{2,1,0:T(8,128)(2,1)}), bf16[128,5,1536]{2,1,0:T(8,128)(2,1)S(1)}, u32[]{:S(2)}, u32[]{:S(2)}) async-start(bf16[128,5,1536]{2,1,0:T(8,128)(2,1)} %bitcast.25), calls=%async_computation | async-start | bytes 6291456 | tf_op jit(solution)/shard_map/all_to_all | solution.py:125
  35.0 71.2 %all-to-all-done = bf16[128,5,1536]{2,1,0:T(8,128)(2,1)S(1)} async-done(((bf16[128,5,1536]{2,1,0:T(8,128)(2,1)}), bf16[128,5,1536]{2,1,0:T(8,128)(2,1)S(1)}, u32[]{:S(2)}, u32[]{:S(2)}) %all-to-all-start) | async-done | bytes 1966112 | tf_op jit(solution)/shard_map/all_to_all | solution.py:125
  109.2 10.4 all-to-all-start.1
  126.0 56.9 %all-to-all-done.1 = bf16[128,5,1536]{2,1,0:T(8,128)(2,1)S(1)} async-done(((bf16[128,5,1536]{2,1,0:T(8,128)(2,1)}), bf16[128,5,1536]{2,1,0:T(8,128)(2,1)S(1)}, u32[]{:S(2)}, u32[]{:S(2)}) %all-to-all-start.1) | async-done | bytes 1966112 | tf_op jit(solution)/shard_map/all_to_all | solution.py:49
  187.3 11.9 %collective-permute-done = bf16[1,32,1536]{2,1,0:T(8,128)(2,1)S(1)} collective-permute-done((bf16[1,32,1536]{2,1,0:T(8,128)(2,1)S(1)}, bf16[1,32,1536]{2,1,0:T(8,128)(2,1)S(1)}, u32[]{:S(2)}, u32[]{:S(2)}) %collective-permute-start) | collective-permute-done | bytes 98336 | tf_op jit(solution)/shard_map/ppermute | solution.py:19
  203.1 7.6 all-to-all-start.2
  210.7 71.7 %all-to-all-done.2 = bf16[128,5,1536]{2,1,0:T(8,128)(2,1)S(1)} async-done(((bf16[128,5,1536]{2,1,0:T(8,128)(2,1)}), bf16[128,5,1536]{2,1,0:T(8,128)(2,1)S(1)}, u32[]{:S(2)}, u32[]{:S(2)}) %all-to-all-start.2) | async-done | bytes 1966112 | tf_op jit(solution)/shard_map/all_to_all | solution.py:125
  282.4 9.1 conditional.6
  284.1 7.4 convolution_convert_fusion.1
  294.3 10.8 all-to-all-start.3
  317.5 58.8 %all-to-all-done.3 = bf16[128,5,1536]{2,1,0:T(8,128)(2,1)S(1)} async-done(((bf16[128,5,1536]{2,1,0:T(8,128)(2,1)}), bf16[128,5,1536]{2,1,0:T(8,128)(2,1)S(1)}, u32[]{:S(2)}, u32[]{:S(2)}) %all-to-all-start.3) | async-done | bytes 1966112 | tf_op jit(solution)/shard_map/all_to_all | solution.py:49
  389.1 7.1 all-to-all-start.4
  396.2 71.7 %all-to-all-done.4 = bf16[128,5,1536]{2,1,0:T(8,128)(2,1)S(1)} async-done(((bf16[128,5,1536]{2,1,0:T(8,128)(2,1)}), bf16[128,5,1536]{2,1,0:T(8,128)(2,1)S(1)}, u32[]{:S(2)}, u32[]{:S(2)}) %all-to-all-start.4) | async-done | bytes 1966112 | tf_op jit(solution)/shard_map/all_to_all | solution.py:125
  467.9 9.1 conditional.7
  469.6 7.4 convolution_convert_fusion.2
  479.8 10.6 all-to-all-start.5
  494.8 66.8 %all-to-all-done.5 = bf16[128,5,1536]{2,1,0:T(8,128)(2,1)S(1)} async-done(((bf16[128,5,1536]{2,1,0:T(8,128)(2,1)}), bf16[128,5,1536]{2,1,0:T(8,128)(2,1)S(1)}, u32[]{:S(2)}, u32[]{:S(2)}) %all-to-all-start.5) | async-done | bytes 1966112 | tf_op jit(solution)/shard_map/all_to_all | solution.py:49
  565.9 4.6 collective-permute-done.2
  574.4 7.1 all-to-all-start.6
  581.4 71.7 %all-to-all-done.6 = bf16[128,5,1536]{2,1,0:T(8,128)(2,1)S(1)} async-done(((bf16[128,5,1536]{2,1,0:T(8,128)(2,1)}), bf16[128,5,1536]{2,1,0:T(8,128)(2,1)S(1)}, u32[]{:S(2)}, u32[]{:S(2)}) %all-to-all-start.6) | async-done | bytes 1966112 | tf_op jit(solution)/shard_map/all_to_all | solution.py:125
  653.2 9.1 conditional.8
  654.8 7.4 convolution_convert_fusion.3
  665.1 10.4 all-to-all-start.7
  679.9 66.7 %all-to-all-done.7 = bf16[128,5,1536]{2,1,0:T(8,128)(2,1)S(1)} async-done(((bf16[128,5,1536]{2,1,0:T(8,128)(2,1)}), bf16[128,5,1536]{2,1,0:T(8,128)(2,1)S(1)}, u32[]{:S(2)}, u32[]{:S(2)}) %all-to-all-start.7) | async-done | bytes 1966112 | tf_op jit(solution)/shard_map/all_to_all | solution.py:49
  751.0 4.7 collective-permute-done.3
  759.9 7.2 all-to-all-start.8
  767.5 71.4 %all-to-all-done.8 = bf16[128,5,1536]{2,1,0:T(8,128)(2,1)S(1)} async-done(((bf16[128,5,1536]{2,1,0:T(8,128)(2,1)}), bf16[128,5,1536]{2,1,0:T(8,128)(2,1)S(1)}, u32[]{:S(2)}, u32[]{:S(2)}) %all-to-all-start.8) | async-done | bytes 1966112 | tf_op jit(solution)/shard_map/all_to_all | solution.py:125
  838.9 9.1 conditional.9
  840.6 7.4 convolution_convert_fusion.4
  850.8 10.4 all-to-all-start.9
  872.7 55.6 %all-to-all-done.9 = bf16[128,5,1536]{2,1,0:T(8,128)(2,1)S(1)} async-done(((bf16[128,5,1536]{2,1,0:T(8,128)(2,1)}), bf16[128,5,1536]{2,1,0:T(8,128)(2,1)S(1)}, u32[]{:S(2)}, u32[]{:S(2)}) %all-to-all-start.9) | async-done | bytes 1966112 | tf_op jit(solution)/shard_map/all_to_all | solution.py:49
  936.4 244.1 %all-reduce.3.cloned.1.call-done = (f32[8,256,16]{1,2,0:T(8,128)}, f32[8,256,16]{1,2,0:T(8,128)}) async-done(((f32[8,256,16]{1,2,0:T(8,128)}, f32[8,256,16]{1,2,0:T(8,128)}), (f32[8,256,16]{1,2,0:T(8,128)}, f32[8,256,16]{1,2,0:T(8,128)})) %all-reduce.3.cloned.1.call-update) | async-done | bytes 262160 | tf_op jit(solution)/shard_map/psum | solution.py:169
  (384 shorter events, 118.2 us)
Async XLA Ops:
  15.1 108.8 %copy-start.63 = (s32[1,1,32,2]{2,3,1,0:T(2,128)}, s32[1,1,32,2]{2,3,1,0:T(2,128)S(1)}, u32[]{:S(2)}) copy-start(s32[1,1,32,2]{2,3,1,0:T(2,128)S(1)} %get-tuple-element.168) | copy-start | bytes 772
  18.7 87.6 %all-to-all-start = ((bf16[128,5,1536]{2,1,0:T(8,128)(2,1)}), bf16[128,5,1536]{2,1,0:T(8,128)(2,1)S(1)}, u32[]{:S(2)}, u32[]{:S(2)}) async-start(bf16[128,5,1536]{2,1,0:T(8,128)(2,1)} %bitcast.25), calls=%async_computation | async-start | bytes 6291456 | tf_op jit(solution)/shard_map/all_to_all | solution.py:125
  109.2 73.8 %all-to-all-start.1 = ((bf16[128,5,1536]{2,1,0:T(8,128)(2,1)}), bf16[128,5,1536]{2,1,0:T(8,128)(2,1)S(1)}, u32[]{:S(2)}, u32[]{:S(2)}) async-start(bf16[128,5,1536]{2,1,0:T(8,128)(2,1)} %copy.130), calls=%async_computation.1 | async-start | bytes 6291456 | tf_op jit(solution)/shard_map/all_to_all | solution.py:49
  126.0 57.6 %copy-start.42 = (f32[1536]{0:T(1024)S(1)}, f32[1536]{0:T(1024)}, u32[]{:S(2)}) copy-start(f32[1536]{0:T(1024)} %get-tuple-element.111) | copy-start | bytes 18436
  126.0 73.2 %copy-start.18 = (f32[32,768]{1,0:T(8,128)S(1)}, f32[32,768]{1,0:T(8,128)}, u32[]{:S(2)}) copy-start(f32[32,768]{1,0:T(8,128)} %get-tuple-element.157) | copy-start | bytes 294916
  126.0 73.2 %copy-start.40 = (f32[1536]{0:T(1024)S(1)}, f32[1536]{0:T(1024)}, u32[]{:S(2)}) copy-start(f32[1536]{0:T(1024)} %get-tuple-element.96) | copy-start | bytes 18436
  183.6 17.2 %copy-start.57 = (bf16[16,5,32]{0,1,2:T(8,128)(2,1)S(1)}, bf16[16,5,32]{0,1,2:T(8,128)(2,1)}, u32[]{:S(2)}) copy-start(bf16[16,5,32]{0,1,2:T(8,128)(2,1)} %fusion.164) | copy-start | bytes 15364
  185.4 13.8 %collective-permute-start = (bf16[1,32,1536]{2,1,0:T(8,128)(2,1)S(1)}, bf16[1,32,1536]{2,1,0:T(8,128)(2,1)S(1)}, u32[]{:S(2)}, u32[]{:S(2)}) collective-permute-start(bf16[1,32,1536]{2,1,0:T(8,128)(2,1)S(1)} %bitcast.428), channel_id=1, source_target_pairs={{0,128},{1,129},{2,130},{3,131},{4,132},{5,133},{6,134},{7,135},{8... | collective-permute-start | bytes 294920 | tf_op jit(solution)/shard_map/ppermute | solution.py:19
  203.1 79.3 %all-to-all-start.2 = ((bf16[128,5,1536]{2,1,0:T(8,128)(2,1)}), bf16[128,5,1536]{2,1,0:T(8,128)(2,1)S(1)}, u32[]{:S(2)}, u32[]{:S(2)}) async-start(bf16[128,5,1536]{2,1,0:T(8,128)(2,1)} %bitcast.48), calls=%async_computation.2 | async-start | bytes 6291456 | tf_op jit(solution)/shard_map/all_to_all | solution.py:125
  294.3 82.0 %all-to-all-start.3 = ((bf16[128,5,1536]{2,1,0:T(8,128)(2,1)}), bf16[128,5,1536]{2,1,0:T(8,128)(2,1)S(1)}, u32[]{:S(2)}, u32[]{:S(2)}) async-start(bf16[128,5,1536]{2,1,0:T(8,128)(2,1)} %copy.141), calls=%async_computation.3 | async-start | bytes 6291456 | tf_op jit(solution)/shard_map/all_to_all | solution.py:49
  317.5 59.4 %copy-start.43 = (f32[1536]{0:T(1024)S(1)}, f32[1536]{0:T(1024)}, u32[]{:S(2)}) copy-start(f32[1536]{0:T(1024)} %get-tuple-element.108) | copy-start | bytes 18436
  317.5 67.8 %copy-start.12 = (f32[32,768]{1,0:T(8,128)S(1)}, f32[32,768]{1,0:T(8,128)}, u32[]{:S(2)}) copy-start(f32[32,768]{1,0:T(8,128)} %get-tuple-element.159) | copy-start | bytes 294916
  317.5 67.8 %copy-start.39 = (f32[1536]{0:T(1024)S(1)}, f32[1536]{0:T(1024)}, u32[]{:S(2)}) copy-start(f32[1536]{0:T(1024)} %get-tuple-element.95) | copy-start | bytes 18436
  378.8 6.5 collective-permute-start.1
  389.1 78.8 %all-to-all-start.4 = ((bf16[128,5,1536]{2,1,0:T(8,128)(2,1)}), bf16[128,5,1536]{2,1,0:T(8,128)(2,1)S(1)}, u32[]{:S(2)}, u32[]{:S(2)}) async-start(bf16[128,5,1536]{2,1,0:T(8,128)(2,1)} %bitcast.70), calls=%async_computation.4 | async-start | bytes 6291456 | tf_op jit(solution)/shard_map/all_to_all | solution.py:125
  479.8 81.8 %all-to-all-start.5 = ((bf16[128,5,1536]{2,1,0:T(8,128)(2,1)}), bf16[128,5,1536]{2,1,0:T(8,128)(2,1)S(1)}, u32[]{:S(2)}, u32[]{:S(2)}) async-start(bf16[128,5,1536]{2,1,0:T(8,128)(2,1)} %copy.152), calls=%async_computation.5 | async-start | bytes 6291456 | tf_op jit(solution)/shard_map/all_to_all | solution.py:49
  494.8 75.8 %copy-start.10 = (f32[32,768]{1,0:T(8,128)S(1)}, f32[32,768]{1,0:T(8,128)}, u32[]{:S(2)}) copy-start(f32[32,768]{1,0:T(8,128)} %get-tuple-element.161) | copy-start | bytes 294916
  494.8 75.8 %copy-start.11 = (f32[32,768]{1,0:T(8,128)S(1)}, f32[32,768]{1,0:T(8,128)}, u32[]{:S(2)}) copy-start(f32[32,768]{1,0:T(8,128)} %get-tuple-element.162) | copy-start | bytes 294916
  494.8 75.8 %copy-start.38 = (f32[1536]{0:T(1024)S(1)}, f32[1536]{0:T(1024)}, u32[]{:S(2)}) copy-start(f32[1536]{0:T(1024)} %get-tuple-element.98) | copy-start | bytes 18436
  564.0 6.5 collective-permute-start.2
  574.4 78.8 %all-to-all-start.6 = ((bf16[128,5,1536]{2,1,0:T(8,128)(2,1)}), bf16[128,5,1536]{2,1,0:T(8,128)(2,1)S(1)}, u32[]{:S(2)}, u32[]{:S(2)}) async-start(bf16[128,5,1536]{2,1,0:T(8,128)(2,1)} %bitcast.92), calls=%async_computation.6 | async-start | bytes 6291456 | tf_op jit(solution)/shard_map/all_to_all | solution.py:125
  665.1 81.5 %all-to-all-start.7 = ((bf16[128,5,1536]{2,1,0:T(8,128)(2,1)}), bf16[128,5,1536]{2,1,0:T(8,128)(2,1)S(1)}, u32[]{:S(2)}, u32[]{:S(2)}) async-start(bf16[128,5,1536]{2,1,0:T(8,128)(2,1)} %copy.163), calls=%async_computation.7 | async-start | bytes 6291456 | tf_op jit(solution)/shard_map/all_to_all | solution.py:49
  679.9 75.8 %copy-start.8 = (f32[32,768]{1,0:T(8,128)S(1)}, f32[32,768]{1,0:T(8,128)}, u32[]{:S(2)}) copy-start(f32[32,768]{1,0:T(8,128)} %get-tuple-element.147) | copy-start | bytes 294916
  679.9 75.8 %copy-start.9 = (f32[32,768]{1,0:T(8,128)S(1)}, f32[32,768]{1,0:T(8,128)}, u32[]{:S(2)}) copy-start(f32[32,768]{1,0:T(8,128)} %get-tuple-element.148) | copy-start | bytes 294916
  679.9 75.8 %copy-start.37 = (f32[1536]{0:T(1024)S(1)}, f32[1536]{0:T(1024)}, u32[]{:S(2)}) copy-start(f32[1536]{0:T(1024)} %get-tuple-element.94) | copy-start | bytes 18436
  749.1 6.6 collective-permute-start.3
  759.9 79.0 %all-to-all-start.8 = ((bf16[128,5,1536]{2,1,0:T(8,128)(2,1)}), bf16[128,5,1536]{2,1,0:T(8,128)(2,1)S(1)}, u32[]{:S(2)}, u32[]{:S(2)}) async-start(bf16[128,5,1536]{2,1,0:T(8,128)(2,1)} %bitcast.114), calls=%async_computation.8 | async-start | bytes 6291456 | tf_op jit(solution)/shard_map/all_to_all | solution.py:125
  850.8 77.5 %all-to-all-start.9 = ((bf16[128,5,1536]{2,1,0:T(8,128)(2,1)}), bf16[128,5,1536]{2,1,0:T(8,128)(2,1)S(1)}, u32[]{:S(2)}, u32[]{:S(2)}) async-start(bf16[128,5,1536]{2,1,0:T(8,128)(2,1)} %copy.174), calls=%async_computation.9 | async-start | bytes 6291456 | tf_op jit(solution)/shard_map/all_to_all | solution.py:49
  861.2 319.3 %all-reduce.3.cloned.1.call-start = ((), (), s32[]{:S(2)}) async-start(), calls=%async_computation.10 | async-start | bytes 524288 | tf_op jit(solution)/shard_map/psum | solution.py:169
  872.7 56.2 %copy-start.41 = (f32[1536]{0:T(1024)S(1)}, f32[1536]{0:T(1024)}, u32[]{:S(2)}) copy-start(f32[1536]{0:T(1024)} %get-tuple-element.99) | copy-start | bytes 18436
  872.7 57.5 %copy-start.25 = (f32[4,32,16]{1,2,0:T(8,128)S(1)}, f32[4,32,16]{1,2,0:T(8,128)}, u32[]{:S(2)}) copy-start(f32[4,32,16]{1,2,0:T(8,128)} %copy-done.24) | copy-start | bytes 24580
  872.7 61.1 %copy-start.26 = (f32[4,32,16]{1,2,0:T(8,128)S(1)}, f32[4,32,16]{1,2,0:T(8,128)}, u32[]{:S(2)}) copy-start(f32[4,32,16]{1,2,0:T(8,128)} %param.21) | copy-start | bytes 24580
  (76 other events, 397.2 us)
Sparse Core Ops, SparseCore 0:
  936.5 243.9 all-reduce.2
where the time goes:
time: 1200 us; the launch traced here: 1190 us
  waiting for transfers between devices  932 us (78%)
  starting transfers between devices  103 us (9%)
  matrix products  61.5 us (5%)
  local copies, waits for them, and re-layouts  51.1 us (4%)
  other arithmetic  21.9 us (2%)
  between operations  16 us (1%)
    all_to_all x5, waiting for transfers between devices, local(): lax.all_to_all(outgoing, 'expert', split_axis=0, concat_axis=0, tiled=True)  358 us
    all_to_all x5, waiting for transfers between devices, make_expert(): lax.all_to_all(partial_value, 'expert', split_axis=0, concat_axis=0, tile...  305 us
    psum x1, waiting for transfers between devices, local(): map_total, square_sum = lax.psum((map_sum, map_sq), ('segment', 'expert'))  244 us
    all_to_all x5, starting transfers between devices, make_expert(): lax.all_to_all(partial_value, 'expert', split_axis=0, concat_axis=0, tile...  52.5 us
    all_to_all x5, starting transfers between devices, local(): lax.all_to_all(outgoing, 'expert', split_axis=0, concat_axis=0, tiled=True)  45.3 us
    dot_general x4, matrix products, compute(): jnp.einsum('skh,hd->skd', inner_act, w_second, preferred_element_type=jnp...  29.7 us
    ppermute x4, waiting for transfers between devices, from_behind(): return lax.ppermute(block, axis, route)  25.8 us
  transfers between devices with their start and end apart: 15, of which 15 were waited for; matrix products, arithmetic and copies ran while one was open for 3% of the time, Pallas kernels for 0%

commit v1 on v0

v1 whole, which is shorter than its diff:
```python
import functools

import jax
import jax.numpy as jnp
from jax import lax
from jax.experimental import pallas as pl
from jax.experimental.pallas import tpu as pltpu
from jax.sharding import PartitionSpec as P

SAMPLES = 8
SEQ = 256
CAP = 5
PAD = 8

epsilon = 1e-06
time_step = 0.25
time_left = 0.5

f32 = jnp.float32
bf16 = jnp.bfloat16
MESH = pl.DeviceIdType.MESH


def normalize(values_in):
    centered = values_in - jnp.mean(values_in, axis=-1, keepdims=True)
    variance = jnp.mean(centered * centered, axis=-1, keepdims=True)
    return centered * lax.rsqrt(variance + epsilon)


def dot(left, right):
    return jnp.dot(left, right, preferred_element_type=f32)


def position_table(positions, model_width):
    half_width = model_width // 2
    frequency = jnp.exp(-jnp.log(10000.0) * jnp.arange(half_width, dtype=f32) / half_width)
    angles = positions.astype(f32)[:, None] * frequency[None, :]
    return jnp.concatenate([jnp.sin(angles), jnp.cos(angles)], axis=-1)


def kernel(
    sizes,
    hidden_in, latents_in, w_final, choice_in, spread_in, modulation, router_in, w_first, w_second,
    next_out, mean_out, var_out,
    hid, mix, choice, spread, mods, router, first, second,
    out_send, out_recv, rows_in, rows_out, parts, home_send, home_recv,
    stats, stats_recv, maps, send_sems, recv_sems, load_sems, push_sems, land_sems,
):
    groups, members, samples, rows, width, flat = sizes
    half = members // 2
    group_rows = groups * CAP
    core = lax.axis_index("segment")
    device = lax.axis_index("expert")
    group, member = device // members, device % members
    prompt_half, sample = group // samples, group % samples
    halves = groups // samples
    other = 1 - core

    def expert_at(to_group, to_member):
        return {"expert": to_group * members + to_member}

    def load_pairs(micro_core):
        pairs = [
            (choice_in.at[pl.ds(2 * micro_core, 2)], choice.at[core]),
            (spread_in.at[pl.ds(2 * micro_core, 2)], spread.at[core]),
            (router_in, router.at[core]),
        ]
        for member_micro in range(2):
            prompt = (2 * micro_core + member_micro) * halves + prompt_half
            pairs.append((modulation.at[0, prompt], mods.at[core, member_micro]))
        pairs.append((w_first.at[0, 0], first.at[core]))
        pairs.append((w_second.at[0, 0], second.at[core]))
        return pairs

    own_loads = [
        pltpu.make_async_copy(src, dst, load_sems.at[i]) for i, (src, dst) in enumerate(load_pairs(core))
    ]
    pushes = [
        pltpu.make_async_remote_copy(
            src_ref=src, dst_ref=dst, send_sem=push_sems.at[i], recv_sem=land_sems.at[i],
            device_id={"segment": other}, device_id_type=MESH,
        )
        for i, (src, dst) in enumerate(load_pairs(other))
    ]
    for copy in own_loads[:5]:
        copy.start()
    for copy in pushes:
        copy.start()
    for copy in own_loads[5:]:
        copy.start()

    slots = groups * PAD
    row_id = lax.broadcasted_iota(jnp.int32, (group_rows, slots), 0)
    slot_id = lax.broadcasted_iota(jnp.int32, (group_rows, slots), 1)
    within = slot_id & (PAD - 1)
    packing = jnp.where((row_id == CAP * (slot_id >> 3) + within) & (within < CAP), 1.0, 0.0).astype(bf16)
    row_id_t = lax.broadcasted_iota(jnp.int32, (slots, group_rows), 1)
    slot_id_t = lax.broadcasted_iota(jnp.int32, (slots, group_rows), 0)
    within_t = slot_id_t & (PAD - 1)
    unpacking = jnp.where(
        (row_id_t == CAP * (slot_id_t >> 3) + within_t) & (within_t < CAP), 1.0, 0.0
    ).astype(bf16)

    def wait_bytes(ref, sem):
        pltpu.make_async_copy(ref, ref, sem).wait()

    def send_across(unit, source, target, stage):
        target[unit, group] = source[unit, group]

        @pl.loop(1, groups)
        def _(k):
            to_group = (group + k) % groups
            pltpu.make_async_remote_copy(
                src_ref=source.at[unit, to_group], dst_ref=target.at[unit, group],
                send_sem=send_sems.at[stage, unit], recv_sem=recv_sems.at[stage, unit],
                device_id=expert_at(to_group, member), device_id_type=MESH,
            ).start()

    def front(layer, micro):
        unit = 2 * layer + micro
        shift, scale = mods[layer, micro, 0:1], mods[layer, micro, 1:2]
        normed = (normalize(hid[micro].astype(f32)) * (1.0 + scale) + shift).astype(bf16)
        logits = dot(normed, router[layer])
        hot_0, hot_1 = choice[layer, micro, 0].astype(f32), choice[layer, micro, 1].astype(f32)
        prob_0 = lax.logistic(jnp.sum(hot_0 * logits, axis=1, keepdims=True))
        prob_1 = lax.logistic(jnp.sum(hot_1 * logits, axis=1, keepdims=True))
        weights = (hot_0 * prob_0 + hot_1 * prob_1) / (prob_0 + prob_1)
        mix[micro] = weights
        packed = dot(spread[layer, micro], normed)
        out_send[unit] = packed.reshape(groups, PAD, width).astype(bf16)
        send_across(unit, out_send, out_recv, 0)

    def gather(layer, micro):
        unit = 2 * layer + micro
        wait_bytes(out_recv.at[unit, pl.ds(0, groups - 1)], recv_sems.at[0, unit])
        arrived = out_recv[unit].astype(f32).reshape(slots, width).astype(bf16)
        rows_in[unit, member] = dot(packing, arrived).astype(bf16)

        @pl.loop(1, members)
        def _(k):
            to_member = (member + k) % members
            pltpu.make_async_remote_copy(
                src_ref=rows_in.at[unit, member], dst_ref=rows_in.at[unit, member],
                send_sem=send_sems.at[1, unit], recv_sem=recv_sems.at[1, unit],
                device_id=expert_at(group, to_member), device_id_type=MESH,
            ).start()

    def compute(layer, micro):
        unit = 2 * layer + micro
        wait_bytes(rows_in.at[unit, pl.ds(0, members - 1)], recv_sems.at[1, unit])

        @pl.loop(0, 2)
        def _(step):
            plane = (member // half + 1 + step) % 2
            block = pl.ds(plane * half, half)
            inner = dot(rows_in[unit, block].reshape(half * group_rows, width), first[layer])
            inner = jax.nn.gelu(inner, approximate=True).astype(bf16)
            partial = dot(inner, second[layer]).astype(bf16)
            rows_out[unit, block] = partial.reshape(half, group_rows, width)

            @pl.loop(0, half)
            def _(k):
                to_member = plane * half + (member + k) % half

                @pl.when(to_member != member)
                def _():
                    pltpu.make_async_remote_copy(
                        src_ref=rows_out.at[unit, to_member], dst_ref=parts.at[unit, member],
                        send_sem=send_sems.at[2, unit], recv_sem=recv_sems.at[2, unit],
                        device_id=expert_at(group, to_member), device_id_type=MESH,
                    ).start()

        parts[unit, member] = rows_out[unit, member]

    def send_home(layer, micro):
        unit = 2 * layer + micro
        wait_bytes(parts.at[unit, pl.ds(0, members - 1)], recv_sems.at[2, unit])
        total = parts[unit, 0].astype(f32)
        for k in range(1, members):
            total = total + parts[unit, k].astype(f32)
        spaced = dot(unpacking, total.astype(bf16))
        home_send[unit] = spaced.reshape(groups, PAD, width).astype(bf16)
        send_across(unit, home_send, home_recv, 3)

    def combine(layer, micro):
        unit = 2 * layer + micro
        wait_bytes(home_recv.at[unit, pl.ds(0, groups - 1)], recv_sems.at[3, unit])
        returned = home_recv[unit].astype(f32).reshape(slots, width).astype(bf16)
        weights = mix[micro]
        coarse = weights.astype(bf16)
        fine = (weights - coarse.astype(f32)).astype(bf16)
        moe = dot(coarse, returned) + dot(fine, returned)
        hid[micro] = (hid[micro].astype(f32) + mods[layer, micro, 2:3] * moe).astype(bf16)

    hid[...] = hidden_in[...]

    for copy in own_loads[:5]:
        copy.wait()
    for copy in pushes[:5]:
        copy.wait_recv()

    for micro in range(2):
        front(0, micro)

    @pl.loop(0, 2)
    def _(layer):
        @pl.loop(0, 2)
        def _(micro):
            gather(layer, micro)

        @pl.when(layer == 0)
        def _():
            for copy in own_loads[5:]:
                copy.wait()
            for copy in pushes[5:]:
                copy.wait_recv()

        @pl.loop(0, 2)
        def _(micro):
            compute(layer, micro)

        @pl.loop(0, 2)
        def _(micro):
            send_home(layer, micro)

        @pl.loop(0, 2)
        def _(micro):
            combine(layer, micro)

            @pl.when(layer == 0)
            def _():
                front(1, micro)

    lane = lax.broadcasted_iota(jnp.int32, (rows, 128), 1)
    row = lax.broadcasted_iota(jnp.int32, (rows, 128), 0)
    kept = (lane >> 4) == (row & 7)
    for micro in range(2):
        final = normalize(hid[micro].astype(f32)).astype(bf16)
        velocity = jnp.where(kept, dot(final, w_final[...]), 0.0)
        velocity = jnp.sum(velocity.reshape(flat, 8, 128), axis=1)
        start = latents_in[micro]
        next_out[micro] = start + time_step * velocity
        clean = start + time_left * velocity
        stats[pl.ds(2 * micro * flat, flat)] = clean
        stats[pl.ds((2 * micro + 1) * flat, flat)] = clean * clean

    stats_recv[sample] = stats[...]

    @pl.loop(1, samples)
    def _(k):
        to_sample = (sample + k) % samples
        pltpu.make_async_remote_copy(
            src_ref=stats, dst_ref=stats_recv.at[sample],
            send_sem=push_sems.at[7], recv_sem=land_sems.at[7],
            device_id=expert_at(prompt_half * samples + to_sample, member), device_id_type=MESH,
        ).start()

    wait_bytes(stats_recv.at[pl.ds(0, samples - 1)], land_sems.at[7])
    total = stats_recv[0]
    for k in range(1, samples):
        total = total + stats_recv[k]
    keys = 2 * halves * members
    key = (core * halves + prompt_half) * members + member
    maps[key] = total

    @pl.loop(1, keys)
    def _(k):
        to_key = (key + k) % keys
        to_core = to_key // (halves * members)
        to_half = (to_key // members) % halves
        pltpu.make_async_remote_copy(
            src_ref=maps.at[key], dst_ref=maps.at[key],
            send_sem=push_sems.at[8], recv_sem=land_sems.at[8],
            device_id={
                "segment": to_core, "expert": (to_half * samples + sample) * members + to_key % members
            },
            device_id_type=MESH,
        ).start()

    wait_bytes(maps.at[pl.ds(0, keys - 1)], land_sems.at[8])
    for from_key in range(keys):
        from_core, from_half, from_member = (
            from_key // (halves * members), (from_key // members) % halves, from_key % members
        )
        for micro in range(2):
            prompt = (2 * from_core + micro) * halves + from_half
            place = pl.ds(from_member * flat, flat)
            mean = maps[from_key, pl.ds(2 * micro * flat, flat)] / SAMPLES
            square = maps[from_key, pl.ds((2 * micro + 1) * flat, flat)] / SAMPLES
            mean_out[prompt, place] = mean
            var_out[prompt, place] = square - mean * mean

    for copy in pushes:
        copy.wait_send()
    wait_bytes(stats_recv.at[pl.ds(0, samples - 1)], push_sems.at[7])
    wait_bytes(maps.at[pl.ds(0, keys - 1)], push_sems.at[8])

    @pl.loop(0, 4)
    def _(unit):
        wait_bytes(out_recv.at[unit, pl.ds(0, groups - 1)], send_sems.at[0, unit])
        wait_bytes(rows_in.at[unit, pl.ds(0, members - 1)], send_sems.at[1, unit])
        wait_bytes(parts.at[unit, pl.ds(0, members - 1)], send_sems.at[2, unit])
        wait_bytes(home_recv.at[unit, pl.ds(0, groups - 1)], send_sems.at[3, unit])


def local(latents, cond, w_embed, modulation, router, w_in, w_out, routes, w_final):
    core = lax.axis_index("segment")
    device = lax.axis_index("expert")
    devices = lax.axis_size("expert")
    micro_count, rows, patch = latents.shape
    width, experts = router.shape[1], router.shape[2]
    hidden_slice = w_in.shape[3]
    members = devices // experts
    groups = experts
    rows_all = rows * devices
    flat = rows * patch // 128
    slots = groups * PAD
    group_rows = groups * CAP
    prompts = cond.shape[0]

    own = lax.dynamic_slice_in_dim(latents, 2 * core, 2, 0)
    row_start = (2 * core + jnp.arange(2)) * rows_all + device * rows
    prompt = row_start // (SEQ * SAMPLES)
    positions = (device * rows) % SEQ + jnp.arange(rows, dtype=jnp.int32)
    embedded = jnp.einsum("mrp,pd->mrd", own, w_embed, precision=lax.Precision.HIGHEST)
    cond_rows = jnp.stack([lax.dynamic_index_in_dim(cond, prompt[i], 0, keepdims=True) for i in range(2)])
    hidden = (embedded + position_table(positions, width) + cond_rows).astype(bf16)

    chosen = routes[0]
    hot = (chosen[..., None] == jnp.arange(experts, dtype=jnp.int32)).astype(bf16)
    earlier = jnp.tril(jnp.ones((rows, rows), bf16), -1)
    before = jnp.einsum("rs,mse->mre", earlier, hot[:, :, 0] + hot[:, :, 1], preferred_element_type=f32)
    slot = jnp.sum(before[:, :, None, :] * hot.astype(f32), axis=3).astype(jnp.int32)
    place = (chosen * PAD + slot).transpose(0, 2, 1)
    choice = (place[..., None] == jnp.arange(slots, dtype=jnp.int32)).astype(bf16)
    spread = (
        (place[:, 0, None, :] == jnp.arange(slots, dtype=jnp.int32)[:, None])
        | (place[:, 1, None, :] == jnp.arange(slots, dtype=jnp.int32)[:, None])
    ).astype(bf16)

    vmem = pl.BlockSpec(memory_space=pltpu.VMEM)
    left = pl.BlockSpec(memory_space=pl.ANY)
    keys = 2 * (groups // SAMPLES) * members
    sizes = (groups, members, SAMPLES, rows, width, flat)
    next_flat, mean_flat, var_flat = pl.pallas_call(
        functools.partial(kernel, sizes),
        out_shape=(
            jax.ShapeDtypeStruct((2, flat, 128), f32),
            jax.ShapeDtypeStruct((prompts, members * flat, 128), f32),
            jax.ShapeDtypeStruct((prompts, members * flat, 128), f32),
        ),
        in_specs=[vmem, vmem, vmem, vmem, vmem, left, vmem, left, left],
        out_specs=(vmem, vmem, vmem),
        scratch_shapes=[
            pltpu.VMEM((2, rows, width), bf16),
            pltpu.VMEM((2, rows, slots), f32),
            pltpu.VMEM((2, 2, 2, rows, slots), bf16),
            pltpu.VMEM((2, 2, slots, rows), bf16),
            pltpu.VMEM((2, 2, 3, width), f32),
            pltpu.VMEM((2, width, slots), bf16),
            pltpu.VMEM((2, width, hidden_slice), bf16),
            pltpu.VMEM((2, hidden_slice, width), bf16),
            pltpu.VMEM((4, groups, PAD, width), bf16),
            pltpu.VMEM((4, groups, PAD, width), bf16),
            pltpu.VMEM((4, members, group_rows, width), bf16),
            pltpu.VMEM((4, members, group_rows, width), bf16),
            pltpu.VMEM((4, members, group_rows, width), bf16),
            pltpu.VMEM((4, groups, PAD, width), bf16),
            pltpu.VMEM((4, groups, PAD, width), bf16),
            pltpu.VMEM((4 * flat, 128), f32),
            pltpu.VMEM((SAMPLES, 4 * flat, 128), f32),
            pltpu.VMEM((keys, 4 * flat, 128), f32),
            pltpu.SemaphoreType.DMA((4, 4)),
            pltpu.SemaphoreType.DMA((4, 4)),
            pltpu.SemaphoreType.DMA((7,)),
            pltpu.SemaphoreType.DMA((9,)),
            pltpu.SemaphoreType.DMA((9,)),
        ],
        compiler_params=pltpu.CompilerParams(has_side_effects=True, vmem_limit_bytes=58 * 1024 * 1024),
        name="flow_step",
    )(
        hidden,
        own.reshape(2, flat, 128),
        jnp.tile(w_final, (1, 128 // patch)),
        choice,
        spread,
        modulation,
        jnp.repeat(router[0], PAD, axis=1),
        w_in,
        w_out,
    )
    return (
        next_flat.reshape(2, rows, patch),
        mean_flat.reshape(prompts, SEQ, patch),
        var_flat.reshape(prompts, SEQ, patch),
    )


def solution(mesh):
    placed = (
        P(None, "expert", None),
        P(),
        P(),
        P("segment", None, None, None),
        P("segment", None, None),
        P("segment", "expert", None, None),
        P("segment", "expert", None, None),
        P("segment", None, "expert", None),
        P(),
    )
    return jax.shard_map(
        local,
        mesh=mesh,
        in_specs=placed,
        out_specs=(P("segment", "expert", None), P(), P()),
        check_vma=False,
    )
```

time: 1200 us -> 339 us (0.28)
  waiting for transfers between devices: 932 us -> 0 us
  Pallas kernels: 0 us -> 318 us
  starting transfers between devices: 103 us -> 0 us
  matrix products: 61.5 us -> 1.38 us
  local copies, waits for them, and re-layouts: 51.1 us -> 11.4 us
  other arithmetic: 21.9 us -> 2.66 us
    all_to_all x10 -> x0, waiting for transfers between devices: 663 us -> none  [the longest x5 358 us: local(): lax.all_to_all(outgoing, 'expert', split_axis=0, concat_axis=0, tiled=True)]
    pallas_call x0 -> x1, Pallas kernels: none -> 318 us  [local(): pl.pallas_call(functools.partial(kernel, sizes), out_shape=(jax.ShapeDtyp...]
    psum x1 -> x0, waiting for transfers between devices: 244 us -> none  [local(): map_total, square_sum = lax.psum((map_sum, map_sq), ('segment', 'expert'))]
    all_to_all x10 -> x0, starting transfers between devices: 97.9 us -> none  [the longest x5 52.5 us: make_expert(): lax.all_to_all(partial_value, 'expert', split_axis=0, concat_axis=0, tile...]
    dot_general x39 -> x2, matrix products: 61.5 us -> 1.38 us  [the longest x1 1.19 us: local(): jnp.einsum('mrp,pd->mrd', own, w_embed, precision=lax.Precision.HIGHEST)]
    ppermute x4 -> x0, waiting for transfers between devices: 25.8 us -> none  [from_behind(): return lax.ppermute(block, axis, route)]
    cond x13 -> x0, local copies, waits for them, and re-layouts: 20.6 us -> none  [the longest x5 13.9 us: make_expert(): partial_value = lax.cond(active, compute, skipped, received)]
  transfers between devices with their start and end apart: 15 -> 0, of which waited for: 15 -> 0; matrix products, arithmetic and copies ran while one was open for 3% -> 0% of each run, Pallas kernels for 0% -> 0%
where the time goes in v1:
time: 339 us; the launch traced here: 338 us
  Pallas kernels  318 us (94%)
  local copies, waits for them, and re-layouts  11.4 us (3%)
  between operations  4.67 us (1%)
    pallas_call x1, Pallas kernels, local(): pl.pallas_call(functools.partial(kernel, sizes), out_shape=(jax.ShapeDtyp...  318 us

profile of v1, /device:TPU:1, one launch (start us, length us, event | category | flops | bytes accessed | tf_op | source)
XLA Modules:
  0.0 338.2 jit_solution(17232994227561793283)
XLA Ops:
  0.6 0.0 copy-start
  0.6 0.0 copy-start.3
  0.7 0.0 copy-start.1
  0.7 0.4 multiply_sine_fusion
  1.2 0.6 fusion.18
  5.6 0.9 dynamic-slice_bitcast_fusion.1
  6.6 0.7 constant_dynamic-slice_fusion
  7.3 0.0 copy-done
  7.3 1.2 fusion.1.hidden_in
  8.5 0.1 copy.28
  8.6 0.7 reshape.40.latents_in
  9.2 0.7 copy.40
  10.0 0.2 convolution_bitcast_fusion
  10.2 0.7 add_bitcast_fusion
  10.9 0.7 fusion.3.spread_in
  11.6 0.7 fusion.4.choice_in
  12.3 0.8 tile.4
  13.1 0.9 copy.31.w_final
  14.1 0.0 copy-done.3
  14.1 0.9 copy.33.router_in
  15.0 0.0 copy-done.1
  15.0 0.8 copy.32.modulation
  15.8 318.1 %flow_step.1 = (f32[2,4,128]{2,1,0:T(4,128)}, f32[8,32,128]{2,1,0:T(8,128)}, f32[8,32,128]{2,1,0:T(8,128)}) custom-call(bf16[2,32,1536]{2,1,0:T(8,128)(2,1)} %fusion.1.hidden_in, f32[2,4,128]{2,1,0:T(4,128)} %reshape.40.latents_in, bf16[1536,128]{1,0:T(8,128)(2,1)} %copy.31.w_final, bf16[4,2,32,128]{3,2,1,0:T(8,128)(2,1)} %fusion.4.choice_in, ...), custom_call_target="tpu_custom_call" | custom-call | tf_op jit(solution)/shard_map/flow_step/pallas_call | solution.py:345
  333.9 0.0 copy-start.2
  333.9 0.0 copy-start.4
  333.9 1.2 reshape.43
  335.2 1.0 copy.35
  336.1 0.0 copy-done.2
  336.1 0.3 reshape.44
  336.5 1.0 copy.36
  337.4 0.1 reshape.42
  337.5 0.7 copy.34
  (12 shorter events, 0.2 us)
Async XLA Ops:
  0.6 6.7 %copy-start = (f32[16,1536]{1,0:T(8,128)S(1)}, f32[16,1536]{1,0:T(8,128)}, u32[]{:S(2)}) copy-start(f32[16,1536]{1,0:T(8,128)} %param.11) | copy-start | bytes 294916
  0.6 13.4 %copy-start.3 = (bf16[1,1536,16]{1,2,0:T(8,128)(2,1)S(1)}, bf16[1,1536,16]{1,2,0:T(8,128)(2,1)}, u32[]{:S(2)}) copy-start(bf16[1,1536,16]{1,2,0:T(8,128)(2,1)} %param.13) | copy-start | bytes 147460
  0.7 14.4 %copy-start.1 = (f32[1,8,3,1536]{3,1,2,0:T(8,128)S(1)}, f32[1,8,3,1536]{3,1,2,0:T(8,128)}, u32[]{:S(2)}) copy-start(f32[1,8,3,1536]{3,1,2,0:T(8,128)} %param.12) | copy-start | bytes 442372
  333.9 2.2 copy-start.2
  333.9 3.5 %copy-start.4 = (f32[2,4,128]{2,1,0:T(4,128)S(1)}, f32[2,4,128]{2,1,0:T(4,128)}, u32[]{:S(2)}) copy-start(f32[2,4,128]{2,1,0:T(4,128)} %get-tuple-element.6) | copy-start | bytes 12292

commit v2 on v1

v2 whole, which is shorter than its diff:
```python
import functools

import jax
import jax.numpy as jnp
from jax import lax
from jax.experimental import pallas as pl
from jax.experimental.pallas import tpu as pltpu
from jax.sharding import PartitionSpec as P

SAMPLES = 8
SEQ = 256
CAP = 5
PAD = 8
Z_FIRST = 640

epsilon = 1e-06
time_step = 0.25
time_left = 0.5

f32 = jnp.float32
bf16 = jnp.bfloat16
MESH = pl.DeviceIdType.MESH


def normalize(values_in):
    centered = values_in - jnp.mean(values_in, axis=-1, keepdims=True)
    variance = jnp.mean(centered * centered, axis=-1, keepdims=True)
    return centered * lax.rsqrt(variance + epsilon)


def dot(left, right, over_left=1, over_right=0, **kwargs):
    dims = (((over_left,), (over_right,)), ((), ()))
    return lax.dot_general(left, right, dims, preferred_element_type=f32, **kwargs)


def iota(shape, dim):
    return lax.broadcasted_iota(jnp.int32, shape, dim)


def kernel(
    sizes,
    latents, cond, w_embed, modulation, router_in, w_first, w_second, routes_in, w_final,
    next_out, mean_out, var_out,
    hid, mix, routes, mods, router, first, second,
    out_send, out_recv, rows_in, rows_out, pair_recv, pair_send, own_recv, line_recv, line_send, cross_recv,
    home_send, home_recv, stats, stats_recv, maps,
    send_sems, recv_sems, load_sems, push_sems, land_sems, map_sems,
):
    groups, members, samples, rows, width, cut = sizes
    half = members // 2
    group_rows = groups * CAP
    slots = groups * PAD
    halves = groups // samples
    keys = 2 * halves * members
    core = lax.axis_index("segment")
    device = lax.axis_index("expert")
    group, member = device // members, device % members
    prompt_half, sample = group // samples, group % samples
    plane, place = member // half, member % half
    far_plane = 1 - plane
    other = 1 - core
    key = (core * halves + prompt_half) * members + member

    def expert_at(to_group, to_member):
        return {"expert": to_group * members + to_member}

    def in_group(to_plane, to_place):
        return expert_at(group, to_plane * half + to_place)

    def key_device(to_key):
        to_core = to_key // (halves * members)
        to_half = (to_key // members) % halves
        return {"segment": to_core, "expert": (to_half * samples + sample) * members + to_key % members}

    left, right = (place + half - 1) % half, (place + 1) % half

    barrier = pltpu.get_barrier_semaphore()

    @pl.loop(1, groups)
    def _(k):
        pl.semaphore_signal(
            barrier, inc=1, device_id=expert_at((group + k) % groups, member), device_id_type=MESH
        )

    @pl.loop(1, members)
    def _(k):
        pl.semaphore_signal(
            barrier, inc=1, device_id=expert_at(group, (member + k) % members), device_id_type=MESH
        )

    @pl.loop(1, keys)
    def _(k):
        pl.semaphore_signal(barrier, inc=1, device_id=key_device((key + k) % keys), device_id_type=MESH)

    def load_pairs(micro_core):
        return [
            (routes_in.at[pl.ds(2 * micro_core, 2)], routes.at[core]),
            (router_in, router.at[core]),
            (modulation, mods.at[core]),
            (w_first.at[0, 0], first.at[core]),
            (w_second.at[0, 0], second.at[core]),
        ]

    own_loads = [
        pltpu.make_async_copy(src, dst, load_sems.at[i]) for i, (src, dst) in enumerate(load_pairs(core))
    ]
    pushes = [
        pltpu.make_async_remote_copy(
            src_ref=src, dst_ref=dst, send_sem=push_sems.at[i], recv_sem=land_sems.at[i],
            device_id={"segment": other}, device_id_type=MESH,
        )
        for i, (src, dst) in enumerate(load_pairs(other))
    ]
    for copy in own_loads:
        copy.start()

    frequency = jnp.exp(
        -jnp.log(jnp.full((1, width // 2), 10000.0, f32))
        * iota((1, width // 2), 1).astype(f32) / (width // 2)
    )
    position = (member * rows + iota((rows, 1), 0)).astype(f32)
    angles = position * frequency
    table = jnp.concatenate([jnp.sin(angles), jnp.cos(angles)], axis=1)
    for micro in range(2):
        prompt = (2 * core + micro) * halves + prompt_half
        embedded = dot(latents[2 * core + micro].T, w_embed[...], precision=lax.Precision.HIGHEST)
        hid[micro] = (embedded + table + cond[pl.ds(prompt, 1)]).astype(bf16)

    def packing(shape, row_dim):
        row, slot = iota(shape, row_dim), iota(shape, 1 - row_dim)
        within = slot & (PAD - 1)
        return jnp.where((row == CAP * (slot >> 3) + within) & (within < CAP), 1.0, 0.0).astype(bf16)

    def wait_bytes(ref, sem):
        pltpu.make_async_copy(ref, ref, sem).wait()

    def send(source, target, send_sem, recv_sem, to):
        pltpu.make_async_remote_copy(
            src_ref=source, dst_ref=target, send_sem=send_sem, recv_sem=recv_sem,
            device_id=to, device_id_type=MESH,
        ).start()

    def send_across(unit, source, target, send_sem, recv_sem):
        target[unit, group] = source[unit, group]

        @pl.loop(1, groups)
        def _(k):
            to_group = (group + k) % groups
            send(
                source.at[unit, to_group], target.at[unit, group], send_sem, recv_sem,
                expert_at(to_group, member),
            )

    def front(layer, micro):
        unit = 2 * layer + micro
        prompt = (2 * core + micro) * halves + prompt_half
        shift, scale = mods[layer, 0, pl.ds(prompt, 1)], mods[layer, 1, pl.ds(prompt, 1)]
        normed = (normalize(hid[micro].astype(f32)) * (1.0 + scale) + shift).astype(bf16)
        logits = dot(router[layer], normed, 1, 1)
        chosen = routes[layer, micro]
        expert = iota((groups, rows), 0)
        slot = iota((slots, rows), 0)
        probs, hots = [], []
        for k in range(2):
            picked = jnp.sum(jnp.where(expert == chosen[k : k + 1], logits, 0.0), axis=0, keepdims=True)
            probs.append(lax.logistic(picked))
            hots.append((slot >> 3) == chosen[k : k + 1])
        both = jnp.where(hots[0] | hots[1], 1.0, 0.0)
        earlier = jnp.where(iota((rows, rows), 0) < iota((rows, rows), 1), 1.0, 0.0).astype(bf16)
        before = dot(both.astype(bf16), earlier)
        match = jnp.where(before == (slot & (PAD - 1)).astype(f32), 1.0, 0.0)
        mix[micro] = (
            jnp.where(hots[0], match, 0.0) * probs[0] + jnp.where(hots[1], match, 0.0) * probs[1]
        ) / (probs[0] + probs[1])
        packed = dot((both * match).astype(bf16), normed)
        out_send[unit] = packed.reshape(groups, PAD, width).astype(bf16)
        send_across(unit, out_send, out_recv, send_sems.at[0, unit], recv_sems.at[0, unit])

    half_width = width // 2

    def gather(layer, micro):
        unit = 2 * layer + micro
        wait_bytes(out_recv.at[unit, pl.ds(0, groups - 1)], recv_sems.at[0, unit])
        arrived = out_recv[unit].astype(f32).reshape(slots, width).astype(bf16)
        rows_in[unit, plane, place] = dot(packing((group_rows, slots), 0), arrived).astype(bf16)
        block = rows_in.at[unit, plane, place]
        send(block, block, send_sems.at[1, unit], recv_sems.at[1, unit], in_group(far_plane, place))
        send(block, block, send_sems.at[1, unit], recv_sems.at[2, unit], in_group(plane, right))
        send(block, block, send_sems.at[1, unit], recv_sems.at[3, unit], in_group(plane, left))

    def relay_across(layer, micro):
        unit = 2 * layer + micro
        block = rows_in.at[unit, far_plane, place]
        wait_bytes(block, recv_sems.at[1, unit])
        send(block, block, send_sems.at[7, unit], recv_sems.at[4, unit], in_group(plane, right))
        send(block, block, send_sems.at[7, unit], recv_sems.at[5, unit], in_group(plane, left))

    def relay_along(unit, of_plane, sem):
        from_left = rows_in.at[unit, of_plane, left]
        from_right = rows_in.at[unit, of_plane, right]
        wait_bytes(from_left, recv_sems.at[sem, unit])
        low = rows_in.at[unit, of_plane, left, :, pl.ds(0, half_width)]
        send(low, low, send_sems.at[7, unit], recv_sems.at[sem + 4, unit], in_group(plane, right))
        wait_bytes(from_right, recv_sems.at[sem + 1, unit])
        high = rows_in.at[unit, of_plane, right, :, pl.ds(half_width, half_width)]
        send(high, high, send_sems.at[7, unit], recv_sems.at[sem + 4, unit], in_group(plane, left))

    def expert(unit, layer, of_plane):
        inner = dot(rows_in[unit, of_plane].reshape(half * group_rows, width), first[layer])
        inner = jax.nn.gelu(inner, approximate=True).astype(bf16)
        partial = dot(inner, second[layer]).astype(bf16)
        rows_out[unit, of_plane] = partial.reshape(half, group_rows, width)

        @pl.loop(1, half)
        def _(k):
            to_place = (place + k) % half
            send(
                rows_out.at[unit, of_plane, to_place, :, pl.ds(cut, width - cut)],
                line_recv.at[unit, place, of_plane],
                send_sems.at[3, unit], recv_sems.at[9, unit], in_group(plane, to_place),
            )

    def compute(layer, micro):
        unit = 2 * layer + micro
        wait_bytes(rows_in.at[unit, far_plane, 0], recv_sems.at[8, unit])

        @pl.loop(0, 2)
        def _(step):
            @pl.when(step == 1)
            def _():
                send(
                    rows_out.at[unit, far_plane, :, :, pl.ds(0, cut)], pair_recv.at[unit],
                    send_sems.at[2, unit], recv_sems.at[7, unit], in_group(far_plane, place),
                )
                wait_bytes(rows_in.at[unit, plane, 0], recv_sems.at[6, unit])

            expert(unit, layer, (far_plane + step) % 2)

        for of_plane in range(2):
            line_recv[unit, place, of_plane] = rows_out[unit, of_plane, place, :, pl.ds(cut, width - cut)]

    def reduce_pair(layer, micro):
        unit = 2 * layer + micro
        wait_bytes(pair_recv.at[unit], recv_sems.at[7, unit])

        @pl.loop(0, half)
        def _(k):
            to_place = (place + 1 + k) % half
            mine = rows_out[unit, plane, to_place, :, pl.ds(0, cut)].astype(f32)
            pair_send[unit, to_place] = (mine + pair_recv[unit, to_place].astype(f32)).astype(bf16)

            @pl.when(k < half - 1)
            def _():
                send(
                    pair_send.at[unit, to_place], own_recv.at[unit, place],
                    send_sems.at[4, unit], recv_sems.at[10, unit], in_group(plane, to_place),
                )

        own_recv[unit, place] = pair_send[unit, place]

    def line_total(unit, of_plane):
        total = line_recv[unit, 0, of_plane].astype(f32)
        for k in range(1, half):
            total = total + line_recv[unit, k, of_plane].astype(f32)
        return total

    def reduce_line(layer, micro):
        unit = 2 * layer + micro
        wait_bytes(line_recv.at[unit, pl.ds(0, half - 1)], recv_sems.at[9, unit])
        line_send[unit] = line_total(unit, far_plane).astype(bf16)
        send(
            line_send.at[unit], cross_recv.at[unit],
            send_sems.at[5, unit], recv_sems.at[11, unit], in_group(far_plane, place),
        )

    def send_home(layer, micro):
        unit = 2 * layer + micro
        wait_bytes(own_recv.at[unit, pl.ds(0, half - 1)], recv_sems.at[10, unit])
        total = own_recv[unit, 0].astype(f32)
        for k in range(1, half):
            total = total + own_recv[unit, k].astype(f32)
        line = line_total(unit, plane)
        wait_bytes(cross_recv.at[unit], recv_sems.at[11, unit])
        line = line + cross_recv[unit].astype(f32)
        unpacking = packing((slots, group_rows), 1)
        spaced = dot(unpacking, jnp.concatenate([total.astype(bf16), line.astype(bf16)], axis=1))
        home_send[unit] = spaced.reshape(groups, PAD, width).astype(bf16)
        send_across(unit, home_send, home_recv, send_sems.at[6, unit], recv_sems.at[12, unit])

    def combine(layer, micro):
        unit = 2 * layer + micro
        wait_bytes(home_recv.at[unit, pl.ds(0, groups - 1)], recv_sems.at[12, unit])
        returned = home_recv[unit].astype(f32).reshape(slots, width).astype(bf16)
        weights = mix[micro].T
        coarse = weights.astype(bf16)
        fine = (weights - coarse.astype(f32)).astype(bf16)
        moe = dot(coarse, returned) + dot(fine, returned)
        prompt = (2 * core + micro) * halves + prompt_half
        gate = mods[layer, 2, pl.ds(prompt, 1)]
        hid[micro] = (hid[micro].astype(f32) + gate * moe).astype(bf16)

    pl.semaphore_wait(barrier, groups - 1 + members - 1 + keys - 1)
    for copy in pushes:
        copy.start()

    for copy in own_loads[:3]:
        copy.wait()
    for copy in pushes[:3]:
        copy.wait_recv()

    for micro in range(2):
        front(0, micro)

    @pl.loop(0, 2)
    def _(layer):
        @pl.loop(0, 2)
        def _(micro):
            gather(layer, micro)

        @pl.loop(0, 2)
        def _(micro):
            relay_across(layer, micro)

        @pl.loop(0, 2)
        def _(micro):
            relay_along(2 * layer + micro, plane, 2)

        @pl.loop(0, 2)
        def _(micro):
            relay_along(2 * layer + micro, far_plane, 4)

        @pl.when(layer == 0)
        def _():
            for copy in own_loads[3:]:
                copy.wait()
            for copy in pushes[3:]:
                copy.wait_recv()

        @pl.loop(0, 2)
        def _(micro):
            compute(layer, micro)

        @pl.loop(0, 2)
        def _(micro):
            reduce_pair(layer, micro)
            reduce_line(layer, micro)

        @pl.loop(0, 2)
        def _(micro):
            send_home(layer, micro)

        @pl.loop(0, 2)
        def _(micro):
            combine(layer, micro)

            @pl.when(layer == 0)
            def _():
                front(1, micro)

    pieces = []
    for micro in range(2):
        final = normalize(hid[micro].astype(f32)).astype(bf16)
        velocity = dot(w_final[...], final, 1, 1)
        start = latents[2 * core + micro]
        next_out[micro] = start + time_step * velocity
        clean = start + time_left * velocity
        pieces += [clean, clean * clean]
    stats[...] = jnp.concatenate(pieces, axis=1)
    stats_recv[sample] = stats[...]

    @pl.loop(1, samples)
    def _(k):
        to_sample = (sample + k) % samples
        send(
            stats, stats_recv.at[sample], map_sems.at[0], map_sems.at[1],
            expert_at(prompt_half * samples + to_sample, member),
        )

    wait_bytes(stats_recv.at[pl.ds(0, samples - 1)], map_sems.at[1])
    total = stats_recv[0]
    for k in range(1, samples):
        total = total + stats_recv[k]
    maps[key] = total

    @pl.loop(1, keys)
    def _(k):
        send(maps.at[key], maps.at[key], map_sems.at[2], map_sems.at[3], key_device((key + k) % keys))

    wait_bytes(maps.at[pl.ds(0, keys - 1)], map_sems.at[3])
    for from_core in range(2):
        for from_half in range(halves):
            blocks = [maps[(from_core * halves + from_half) * members + k] for k in range(members)]
            for micro in range(2):
                prompt = (2 * from_core + micro) * halves + from_half
                lanes = [slice((2 * micro + i) * rows, (2 * micro + i + 1) * rows) for i in range(2)]
                mean = jnp.concatenate([block[:, lanes[0]] for block in blocks], axis=1) / SAMPLES
                square = jnp.concatenate([block[:, lanes[1]] for block in blocks], axis=1) / SAMPLES
                mean_out[prompt] = mean
                var_out[prompt] = square - mean * mean

    for copy in pushes:
        copy.wait_send()
    wait_bytes(stats_recv.at[pl.ds(0, samples - 1)], map_sems.at[0])
    wait_bytes(maps.at[pl.ds(0, keys - 1)], map_sems.at[2])

    @pl.loop(0, 4)
    def _(unit):
        wait_bytes(out_recv.at[unit, pl.ds(0, groups - 1)], send_sems.at[0, unit])
        wait_bytes(out_recv.at[unit, pl.ds(0, groups - 1)], send_sems.at[6, unit])
        wait_bytes(rows_in.at[unit, 0], send_sems.at[7, unit])
        wait_bytes(rows_in.at[unit, 0, pl.ds(0, half - 1)], send_sems.at[1, unit])
        wait_bytes(pair_recv.at[unit], send_sems.at[2, unit])
        wait_bytes(line_recv.at[unit, pl.ds(0, half - 1)], send_sems.at[3, unit])
        wait_bytes(own_recv.at[unit, pl.ds(0, half - 1)], send_sems.at[4, unit])
        wait_bytes(line_send.at[unit], send_sems.at[5, unit])


def local(latents, cond, w_embed, modulation, router, w_in, w_out, routes, w_final):
    devices = lax.axis_size("expert")
    rows, patch = latents.shape[1], latents.shape[2]
    width, groups = router.shape[1], router.shape[2]
    hidden_slice = w_in.shape[3]
    members = devices // groups
    half = members // 2
    slots = groups * PAD
    group_rows = groups * CAP
    prompts = cond.shape[0]
    keys = 2 * (groups // SAMPLES) * members

    vmem = pl.BlockSpec(memory_space=pltpu.VMEM)
    left = pl.BlockSpec(memory_space=pl.ANY)
    sizes = (groups, members, SAMPLES, rows, width, Z_FIRST)
    next_rows, mean_map, var_map = pl.pallas_call(
        functools.partial(kernel, sizes),
        out_shape=(
            jax.ShapeDtypeStruct((2, patch, rows), f32),
            jax.ShapeDtypeStruct((prompts, patch, members * rows), f32),
            jax.ShapeDtypeStruct((prompts, patch, members * rows), f32),
        ),
        in_specs=[vmem, vmem, vmem, left, left, left, left, vmem, vmem],
        out_specs=(vmem, vmem, vmem),
        scratch_shapes=[
            pltpu.VMEM((2, rows, width), bf16),
            pltpu.VMEM((2, slots, rows), f32),
            pltpu.VMEM((2, 2, 2, rows), jnp.int32),
            pltpu.VMEM((2, 3, prompts, width), f32),
            pltpu.VMEM((2, groups, width), bf16),
            pltpu.VMEM((2, width, hidden_slice), bf16),
            pltpu.VMEM((2, hidden_slice, width), bf16),
            pltpu.VMEM((4, groups, PAD, width), bf16),
            pltpu.VMEM((4, groups, PAD, width), bf16),
            pltpu.VMEM((4, 2, half, group_rows, width), bf16),
            pltpu.VMEM((4, 2, half, group_rows, width), bf16),
            pltpu.VMEM((4, half, group_rows, Z_FIRST), bf16),
            pltpu.VMEM((4, half, group_rows, Z_FIRST), bf16),
            pltpu.VMEM((4, half, group_rows, Z_FIRST), bf16),
            pltpu.VMEM((4, half, 2, group_rows, width - Z_FIRST), bf16),
            pltpu.VMEM((4, group_rows, width - Z_FIRST), bf16),
            pltpu.VMEM((4, group_rows, width - Z_FIRST), bf16),
            pltpu.VMEM((4, groups, PAD, width), bf16),
            pltpu.VMEM((4, groups, PAD, width), bf16),
            pltpu.VMEM((patch, 4 * rows), f32),
            pltpu.VMEM((SAMPLES, patch, 4 * rows), f32),
            pltpu.VMEM((keys, patch, 4 * rows), f32),
            pltpu.SemaphoreType.DMA((8, 4)),
            pltpu.SemaphoreType.DMA((13, 4)),
            pltpu.SemaphoreType.DMA((5,)),
            pltpu.SemaphoreType.DMA((5,)),
            pltpu.SemaphoreType.DMA((5,)),
            pltpu.SemaphoreType.DMA((4,)),
        ],
        compiler_params=pltpu.CompilerParams(
            has_side_effects=True, collective_id=0, vmem_limit_bytes=58 * 1024 * 1024
        ),
        name="flow_step",
    )(
        latents.transpose(0, 2, 1),
        cond,
        w_embed,
        modulation[0].transpose(1, 0, 2),
        router[0].T,
        w_in,
        w_out,
        routes[0].transpose(0, 2, 1),
        w_final.T,
    )
    return (next_rows.transpose(0, 2, 1), mean_map.transpose(0, 2, 1), var_map.transpose(0, 2, 1))


def solution(mesh):
    placed = (
        P(None, "expert", None),
        P(),
        P(),
        P("segment", None, None, None),
        P("segment", None, None),
        P("segment", "expert", None, None),
        P("segment", "expert", None, None),
        P("segment", None, "expert", None),
        P(),
    )
    return jax.shard_map(
        local,
        mesh=mesh,
        in_specs=placed,
        out_specs=(P("segment", "expert", None), P(), P()),
        check_vma=False,
    )
```

time: 339 us -> 235 us (0.69)
  Pallas kernels: 318 us -> 230 us
  local copies, waits for them, and re-layouts: 11.4 us -> 4.46 us
  between operations: 4.67 us -> 0.64 us
    pallas_call x1, Pallas kernels: 318 us -> 230 us  [local(): pl.pallas_call(functools.partial(kernel, sizes), out_shape=(jax.ShapeDtyp...]
where the time goes in v2:
time: 235 us
  Pallas kernels  230 us (98%)
  local copies, waits for them, and re-layouts  4.46 us (2%)
    pallas_call x1, Pallas kernels, local(): pl.pallas_call(functools.partial(kernel, sizes), out_shape=(jax.ShapeDtyp...  230 us

profile of v2, /device:TPU:1, one launch (start us, length us, event | category | flops | bytes accessed | tf_op | source)
XLA Modules:
  0.0 234.8 jit_solution(59093807768866425)
XLA Ops:
  0.6 229.7 %flow_step.1 = (f32[2,16,32]{2,1,0:T(8,128)}, f32[8,16,256]{2,1,0:T(8,128)}, f32[8,16,256]{2,1,0:T(8,128)}) custom-call(f32[4,16,32]{2,1,0:T(8,128)} %bitcast.19, f32[8,1536]{1,0:T(8,128)} %cond.1, f32[16,1536]{1,0:T(8,128)} %w_embed.1, f32[3,8,1536]{2,1,0:T(8,128)} %bitcast.14, bf16[16,1536]{1,0:T(8,128)(2,1)} %bitcast.17, ...), custom_call_target="tpu_custom_call" | custom-call | tf_op jit(solution)/shard_map/flow_step/pallas_call | solution.py:433
  230.3 1.3 copy.15
  231.6 1.6 copy.16
  233.2 1.6 copy.17

commit v3 on v2

--- a/solution.py
+++ b/solution.py
@@ -11,7 +11,8 @@
 SEQ = 256
 CAP = 5
 PAD = 8
-Z_FIRST = 640
+Z_FIRST = 896
+ALONG_Y = 1024
 
 epsilon = 1e-06
 time_step = 0.25
@@ -40,13 +41,13 @@
 def kernel(
     sizes,
     latents, cond, w_embed, modulation, router_in, w_first, w_second, routes_in, w_final,
-    next_out, mean_out, var_out,
+    next_out, maps_out,
     hid, mix, routes, mods, router, first, second,
     out_send, out_recv, rows_in, rows_out, pair_recv, pair_send, own_recv, line_recv, line_send, cross_recv,
     home_send, home_recv, stats, stats_recv, maps,
     send_sems, recv_sems, load_sems, push_sems, land_sems, map_sems,
 ):
-    groups, members, samples, rows, width, cut = sizes
+    groups, members, samples, rows, width, cut, along = sizes
     half = members // 2
     group_rows = groups * CAP
     slots = groups * PAD
@@ -126,10 +127,35 @@
         embedded = dot(latents[2 * core + micro].T, w_embed[...], precision=lax.Precision.HIGHEST)
         hid[micro] = (embedded + table + cond[pl.ds(prompt, 1)]).astype(bf16)
 
-    def packing(shape, row_dim):
+    seg = width // 6
+    half_width = width // 2
+
+    def packing(shape, row_dim, part):
         row, slot = iota(shape, row_dim), iota(shape, 1 - row_dim)
-        within = slot & (PAD - 1)
-        return jnp.where((row == CAP * (slot >> 3) + within) & (within < CAP), 1.0, 0.0).astype(bf16)
+        within, start = slot & (PAD - 1), CAP * (slot >> 3)
+        if part < 2:
+            hit = (row == start + (within & 3)) & ((within >> 2) == part)
+        else:
+            hit = (row == start + 4) & (within == part - 2)
+        return jnp.where(hit, 1.0, 0.0).astype(bf16)
+
+    def unpack_rows(low, last, matrix):
+        parts = []
+        for h in range(2):
+            tail = jnp.concatenate([dot(matrix(2 + 3 * h + i), last) for i in range(3)], axis=1)
+            parts.append(dot(matrix(h), low) + tail)
+        return parts
+
+    def pack_rows(full, matrix):
+        low = dot(matrix(0), full[:, :half_width]) + dot(matrix(1), full[:, half_width:])
+        last = dot(matrix(2), full[:, :seg])
+        for i in range(1, 6):
+            last = last + dot(matrix(2 + i), full[:, i * seg : (i + 1) * seg])
+        return jnp.concatenate([low, last], axis=1).reshape(groups, PAD, 4 * seg).astype(bf16)
+
+    def blocks_of(ref, unit):
+        arrived = ref[unit].astype(f32).reshape(slots, 4 * seg).astype(bf16)
+        return arrived[:, :half_width], arrived[:, half_width:]
 
     def wait_bytes(ref, sem):
         pltpu.make_async_copy(ref, ref, sem).wait()
@@ -168,21 +194,28 @@
         both = jnp.where(hots[0] | hots[1], 1.0, 0.0)
         earlier = jnp.where(iota((rows, rows), 0) < iota((rows, rows), 1), 1.0, 0.0).astype(bf16)
         before = dot(both.astype(bf16), earlier)
-        match = jnp.where(before == (slot & (PAD - 1)).astype(f32), 1.0, 0.0)
-        mix[micro] = (
-            jnp.where(hots[0], match, 0.0) * probs[0] + jnp.where(hots[1], match, 0.0) * probs[1]
+        within = slot & (PAD - 1)
+        mix[micro, 0] = (
+            jnp.where(hots[0], probs[0], 0.0) + jnp.where(hots[1], probs[1], 0.0)
         ) / (probs[0] + probs[1])
-        packed = dot((both * match).astype(bf16), normed)
-        out_send[unit] = packed.reshape(groups, PAD, width).astype(bf16)
+        mix[micro, 1] = before
+
+        def spread(part):
+            if part < 2:
+                hit = (before == (within & 3).astype(f32)) & ((within >> 2) == part)
+            else:
+                hit = (before == 4.0) & (within == part - 2)
+            return jnp.where(hit, both, 0.0).astype(bf16)
+
+        out_send[unit] = pack_rows(normed, spread)
         send_across(unit, out_send, out_recv, send_sems.at[0, unit], recv_sems.at[0, unit])
 
-    half_width = width // 2
-
     def gather(layer, micro):
         unit = 2 * layer + micro
         wait_bytes(out_recv.at[unit, pl.ds(0, groups - 1)], recv_sems.at[0, unit])
-        arrived = out_recv[unit].astype(f32).reshape(slots, width).astype(bf16)
-        rows_in[unit, plane, place] = dot(packing((group_rows, slots), 0), arrived).astype(bf16)
+        parts = unpack_rows(*blocks_of(out_recv, unit), lambda part: packing((group_rows, slots), 0, part))
+        for h in range(2):
+            rows_in[unit, plane, place, :, pl.ds(h * half_width, half_width)] = parts[h].astype(bf16)
         block = rows_in.at[unit, plane, place]
         send(block, block, send_sems.at[1, unit], recv_sems.at[1, unit], in_group(far_plane, place))
         send(block, block, send_sems.at[1, unit], recv_sems.at[2, unit], in_group(plane, right))
@@ -190,20 +223,39 @@
 
     def relay_across(layer, micro):
         unit = 2 * layer + micro
-        block = rows_in.at[unit, far_plane, place]
-        wait_bytes(block, recv_sems.at[1, unit])
+        wait_bytes(rows_in.at[unit, far_plane, place], recv_sems.at[1, unit])
+        block = rows_in.at[unit, far_plane, place, :, pl.ds(0, along)]
         send(block, block, send_sems.at[7, unit], recv_sems.at[4, unit], in_group(plane, right))
         send(block, block, send_sems.at[7, unit], recv_sems.at[5, unit], in_group(plane, left))
 
-    def relay_along(unit, of_plane, sem):
-        from_left = rows_in.at[unit, of_plane, left]
-        from_right = rows_in.at[unit, of_plane, right]
-        wait_bytes(from_left, recv_sems.at[sem, unit])
-        low = rows_in.at[unit, of_plane, left, :, pl.ds(0, half_width)]
-        send(low, low, send_sems.at[7, unit], recv_sems.at[sem + 4, unit], in_group(plane, right))
-        wait_bytes(from_right, recv_sems.at[sem + 1, unit])
-        high = rows_in.at[unit, of_plane, right, :, pl.ds(half_width, half_width)]
-        send(high, high, send_sems.at[7, unit], recv_sems.at[sem + 4, unit], in_group(plane, left))
+    def cross(unit, from_place):
+        block = rows_in.at[unit, plane, from_place, :, pl.ds(along, width - along)]
+        send(block, block, send_sems.at[7, unit], recv_sems.at[13, unit], in_group(far_plane, place))
+
+    def relay_own(layer, micro):
+        unit = 2 * layer + micro
+        wait_bytes(rows_in.at[unit, plane, left], recv_sems.at[2, unit])
+        low = rows_in.at[unit, plane, left, :, pl.ds(0, half_width)]
+        send(low, low, send_sems.at[7, unit], recv_sems.at[6, unit], in_group(plane, right))
+        cross(unit, left)
+        wait_bytes(rows_in.at[unit, plane, right], recv_sems.at[3, unit])
+        high = rows_in.at[unit, plane, right, :, pl.ds(half_width, half_width)]
+        send(high, high, send_sems.at[7, unit], recv_sems.at[6, unit], in_group(plane, left))
+        cross(unit, right)
+
+    def relay_far(layer, micro):
+        unit = 2 * layer + micro
+        wait_bytes(rows_in.at[unit, far_plane, left, :, pl.ds(0, along)], recv_sems.at[4, unit])
+        low = rows_in.at[unit, far_plane, left, :, pl.ds(0, along // 2)]
+        send(low, low, send_sems.at[7, unit], recv_sems.at[8, unit], in_group(plane, right))
+        wait_bytes(rows_in.at[unit, far_plane, right, :, pl.ds(0, along)], recv_sems.at[5, unit])
+        high = rows_in.at[unit, far_plane, right, :, pl.ds(along // 2, along // 2)]
+        send(high, high, send_sems.at[7, unit], recv_sems.at[8, unit], in_group(plane, left))
+
+    def relay_opposite(layer, micro):
+        unit = 2 * layer + micro
+        wait_bytes(rows_in.at[unit, plane, 0], recv_sems.at[6, unit])
+        cross(unit, (place + 2) % half)
 
     def expert(unit, layer, of_plane):
         inner = dot(rows_in[unit, of_plane].reshape(half * group_rows, width), first[layer])
@@ -222,20 +274,23 @@
 
     def compute(layer, micro):
         unit = 2 * layer + micro
-        wait_bytes(rows_in.at[unit, far_plane, 0], recv_sems.at[8, unit])
 
         @pl.loop(0, 2)
         def _(step):
             @pl.when(step == 1)
             def _():
-                send(
-                    rows_out.at[unit, far_plane, :, :, pl.ds(0, cut)], pair_recv.at[unit],
-                    send_sems.at[2, unit], recv_sems.at[7, unit], in_group(far_plane, place),
+                wait_bytes(rows_in.at[unit, far_plane, 0, :, pl.ds(0, along)], recv_sems.at[8, unit])
+                wait_bytes(
+                    rows_in.at[unit, far_plane, pl.ds(0, half - 1), :, pl.ds(along, width - along)],
+                    recv_sems.at[13, unit],
                 )
-                wait_bytes(rows_in.at[unit, plane, 0], recv_sems.at[6, unit])
-
-            expert(unit, layer, (far_plane + step) % 2)
-
+
+            expert(unit, layer, (plane + step) % 2)
+
+        send(
+            rows_out.at[unit, far_plane, :, :, pl.ds(0, cut)], pair_recv.at[unit],
+            send_sems.at[2, unit], recv_sems.at[7, unit], in_group(far_plane, place),
+        )
         for of_plane in range(2):
             line_recv[unit, place, of_plane] = rows_out[unit, of_plane, place, :, pl.ds(cut, width - cut)]
 
@@ -282,19 +337,27 @@
         line = line_total(unit, plane)
         wait_bytes(cross_recv.at[unit], recv_sems.at[11, unit])
         line = line + cross_recv[unit].astype(f32)
-        unpacking = packing((slots, group_rows), 1)
-        spaced = dot(unpacking, jnp.concatenate([total.astype(bf16), line.astype(bf16)], axis=1))
-        home_send[unit] = spaced.reshape(groups, PAD, width).astype(bf16)
+        full = jnp.concatenate([total.astype(bf16), line.astype(bf16)], axis=1)
+        home_send[unit] = pack_rows(full, lambda part: packing((slots, group_rows), 1, part))
         send_across(unit, home_send, home_recv, send_sems.at[6, unit], recv_sems.at[12, unit])
 
     def combine(layer, micro):
         unit = 2 * layer + micro
         wait_bytes(home_recv.at[unit, pl.ds(0, groups - 1)], recv_sems.at[12, unit])
-        returned = home_recv[unit].astype(f32).reshape(slots, width).astype(bf16)
-        weights = mix[micro].T
-        coarse = weights.astype(bf16)
-        fine = (weights - coarse.astype(f32)).astype(bf16)
-        moe = dot(coarse, returned) + dot(fine, returned)
+        weights, before = mix[micro, 0].T, mix[micro, 1].T
+        within = iota((rows, slots), 1) & (PAD - 1)
+
+        def weighing(part):
+            if part < 2:
+                hit = (before == (within & 3).astype(f32)) & ((within >> 2) == part)
+            else:
+                hit = (before == 4.0) & (within == part - 2)
+            kept = jnp.where(hit, weights, 0.0)
+            coarse = kept.astype(bf16).astype(f32)
+            return jnp.concatenate([coarse, kept - coarse], axis=0).astype(bf16)
+
+        both = jnp.concatenate(unpack_rows(*blocks_of(home_recv, unit), weighing), axis=1)
+        moe = both[:rows] + both[rows:]
         prompt = (2 * core + micro) * halves + prompt_half
         gate = mods[layer, 2, pl.ds(prompt, 1)]
         hid[micro] = (hid[micro].astype(f32) + gate * moe).astype(bf16)
@@ -323,11 +386,15 @@
 
         @pl.loop(0, 2)
         def _(micro):
-            relay_along(2 * layer + micro, plane, 2)
-
-        @pl.loop(0, 2)
-        def _(micro):
-            relay_along(2 * layer + micro, far_plane, 4)
+            relay_own(layer, micro)
+
+        @pl.loop(0, 2)
+        def _(micro):
+            relay_far(layer, micro)
+
+        @pl.loop(0, 2)
+        def _(micro):
+            relay_opposite(layer, micro)
 
         @pl.when(layer == 0)
         def _():
@@ -387,16 +454,7 @@
         send(maps.at[key], maps.at[key], map_sems.at[2], map_sems.at[3], key_device((key + k) % keys))
 
     wait_bytes(maps.at[pl.ds(0, keys - 1)], map_sems.at[3])
-    for from_core in range(2):
-        for from_half in range(halves):
-            blocks = [maps[(from_core * halves + from_half) * members + k] for k in range(members)]
-            for micro in range(2):
-                prompt = (2 * from_core + micro) * halves + from_half
-                lanes = [slice((2 * micro + i) * rows, (2 * micro + i + 1) * rows) for i in range(2)]
-                mean = jnp.concatenate([block[:, lanes[0]] for block in blocks], axis=1) / SAMPLES
-                square = jnp.concatenate([block[:, lanes[1]] for block in blocks], axis=1) / SAMPLES
-                mean_out[prompt] = mean
-                var_out[prompt] = square - mean * mean
+    maps_out[...] = maps[...]
 
     for copy in pushes:
         copy.wait_send()
@@ -413,6 +471,21 @@
         wait_bytes(line_recv.at[unit, pl.ds(0, half - 1)], send_sems.at[3, unit])
         wait_bytes(own_recv.at[unit, pl.ds(0, half - 1)], send_sems.at[4, unit])
         wait_bytes(line_send.at[unit], send_sems.at[5, unit])
+
+
+def write_out(sizes, maps, next_in, next_out, mean_out, var_out):
+    members, halves, rows = sizes
+    next_out[...] = next_in[...]
+    for core in range(2):
+        for half in range(halves):
+            blocks = [maps[(core * halves + half) * members + k] for k in range(members)]
+            for micro in range(2):
+                prompt = (2 * core + micro) * halves + half
+                lanes = [slice((2 * micro + i) * rows, (2 * micro + i + 1) * rows) for i in range(2)]
+                mean = jnp.concatenate([block[:, lanes[0]] for block in blocks], axis=1) / SAMPLES
+                square = jnp.concatenate([block[:, lanes[1]] for block in blocks], axis=1) / SAMPLES
+                mean_out[prompt] = mean
+                var_out[prompt] = square - mean * mean
 
 
 def local(latents, cond, w_embed, modulation, router, w_in, w_out, routes, w_final):
@@ -429,26 +502,26 @@
 
     vmem = pl.BlockSpec(memory_space=pltpu.VMEM)
     left = pl.BlockSpec(memory_space=pl.ANY)
-    sizes = (groups, members, SAMPLES, rows, width, Z_FIRST)
-    next_rows, mean_map, var_map = pl.pallas_call(
+    block_lanes = 4 * (width // 6)
+    sizes = (groups, members, SAMPLES, rows, width, Z_FIRST, ALONG_Y)
+    next_rows, maps = pl.pallas_call(
         functools.partial(kernel, sizes),
         out_shape=(
             jax.ShapeDtypeStruct((2, patch, rows), f32),
-            jax.ShapeDtypeStruct((prompts, patch, members * rows), f32),
-            jax.ShapeDtypeStruct((prompts, patch, members * rows), f32),
+            jax.ShapeDtypeStruct((keys, patch, 4 * rows), f32),
         ),
         in_specs=[vmem, vmem, vmem, left, left, left, left, vmem, vmem],
-        out_specs=(vmem, vmem, vmem),
+        out_specs=(vmem, vmem),
         scratch_shapes=[
             pltpu.VMEM((2, rows, width), bf16),
-            pltpu.VMEM((2, slots, rows), f32),
+            pltpu.VMEM((2, 2, slots, rows), f32),
             pltpu.VMEM((2, 2, 2, rows), jnp.int32),
             pltpu.VMEM((2, 3, prompts, width), f32),
             pltpu.VMEM((2, groups, width), bf16),
             pltpu.VMEM((2, width, hidden_slice), bf16),
             pltpu.VMEM((2, hidden_slice, width), bf16),
-            pltpu.VMEM((4, groups, PAD, width), bf16),
-            pltpu.VMEM((4, groups, PAD, width), bf16),
+            pltpu.VMEM((4, groups, PAD, block_lanes), bf16),
+            pltpu.VMEM((4, groups, PAD, block_lanes), bf16),
             pltpu.VMEM((4, 2, half, group_rows, width), bf16),
             pltpu.VMEM((4, 2, half, group_rows, width), bf16),
             pltpu.VMEM((4, half, group_rows, Z_FIRST), bf16),
@@ -457,13 +530,13 @@
             pltpu.VMEM((4, half, 2, group_rows, width - Z_FIRST), bf16),
             pltpu.VMEM((4, group_rows, width - Z_FIRST), bf16),
             pltpu.VMEM((4, group_rows, width - Z_FIRST), bf16),
-            pltpu.VMEM((4, groups, PAD, width), bf16),
-            pltpu.VMEM((4, groups, PAD, width), bf16),
+            pltpu.VMEM((4, groups, PAD, block_lanes), bf16),
+            pltpu.VMEM((4, groups, PAD, block_lanes), bf16),
             pltpu.VMEM((patch, 4 * rows), f32),
             pltpu.VMEM((SAMPLES, patch, 4 * rows), f32),
             pltpu.VMEM((keys, patch, 4 * rows), f32),
             pltpu.SemaphoreType.DMA((8, 4)),
-            pltpu.SemaphoreType.DMA((13, 4)),
+            pltpu.SemaphoreType.DMA((14, 4)),
             pltpu.SemaphoreType.DMA((5,)),
             pltpu.SemaphoreType.DMA((5,)),
             pltpu.SemaphoreType.DMA((5,)),
@@ -484,6 +557,17 @@
         routes[0].transpose(0, 2, 1),
         w_final.T,
     )
+    next_rows, mean_map, var_map = pl.pallas_call(
+        functools.partial(write_out, (members, groups // SAMPLES, rows)),
+        out_shape=(
+            jax.ShapeDtypeStruct((2, patch, rows), f32),
+            jax.ShapeDtypeStruct((prompts, patch, members * rows), f32),
+            jax.ShapeDtypeStruct((prompts, patch, members * rows), f32),
+        ),
+        in_specs=[vmem, vmem],
+        out_specs=(vmem, vmem, vmem),
+        name="write_out",
+    )(maps, next_rows)
     return (next_rows.transpose(0, 2, 1), mean_map.transpose(0, 2, 1), var_map.transpose(0, 2, 1))
 
 

time: 235 us -> 198 us (0.84)
  Pallas kernels: 230 us -> 197 us
  local copies, waits for them, and re-layouts: 4.46 us -> 0 us
    pallas_call x1, Pallas kernels: 230 us -> 195 us  [local(): pl.pallas_call(functools.partial(kernel, sizes), out_shape=(jax.ShapeDtyp...]
    unnamed x3 -> x0, local copies, waits for them, and re-layouts: 4.46 us -> none
where the time goes in v3:
time: 198 us
  Pallas kernels  197 us (99%)
    pallas_call x1, Pallas kernels, local(): pl.pallas_call(functools.partial(kernel, sizes), out_shape=(jax.ShapeDtyp...  195 us

profile of v3, /device:TPU:1, one launch (start us, length us, event | category | flops | bytes accessed | tf_op | source)
XLA Modules:
  0.0 197.8 jit_solution(6313745187751800351)
XLA Ops:
  0.6 195.3 %flow_step.1 = (f32[2,16,32]{2,1,0:T(8,128)}, f32[32,16,128]{2,1,0:T(8,128)}) custom-call(f32[4,16,32]{2,1,0:T(8,128)} %bitcast.17, f32[8,1536]{1,0:T(8,128)} %cond.1, f32[16,1536]{1,0:T(8,128)} %w_embed.1, f32[3,8,1536]{2,1,0:T(8,128)} %bitcast.14, bf16[16,1536]{1,0:T(8,128)(2,1)} %bitcast.15, bf16[1,1,1536,768]{3,2,1,0:T(8,128)(2,1)} %w_first.1, ...), custom_call_target="tpu_custom_call" | custom-call | tf_op jit(solution)/shard_map/flow_step/pallas_call | solution.py:507
  195.9 1.9 write_out.1

commit v4 on v3

--- a/solution.py
+++ b/solution.py
@@ -11,7 +11,7 @@
 SEQ = 256
 CAP = 5
 PAD = 8
-Z_FIRST = 896
+Z_FIRST = 768
 ALONG_Y = 1024
 
 epsilon = 1e-06

time: 198 us -> 192 us (0.970)
  Pallas kernels: 197 us -> 192 us
    pallas_call x1, Pallas kernels: 195 us -> 190 us  [local(): pl.pallas_call(functools.partial(kernel, sizes), out_shape=(jax.ShapeDtyp...]
where the time goes in v4:
time: 192 us
  Pallas kernels  192 us (100%)
    pallas_call x1, Pallas kernels, local(): pl.pallas_call(functools.partial(kernel, sizes), out_shape=(jax.ShapeDtyp...  190 us

profile of v4, /device:TPU:1, one launch (start us, length us, event | category | flops | bytes accessed | tf_op | source)
XLA Modules:
  0.0 192.2 jit_solution(16537040965956217317)
XLA Ops:
  0.6 189.7 %flow_step.1 = (f32[2,16,32]{2,1,0:T(8,128)}, f32[32,16,128]{2,1,0:T(8,128)}) custom-call(f32[4,16,32]{2,1,0:T(8,128)} %bitcast.17, f32[8,1536]{1,0:T(8,128)} %cond.1, f32[16,1536]{1,0:T(8,128)} %w_embed.1, f32[3,8,1536]{2,1,0:T(8,128)} %bitcast.14, bf16[16,1536]{1,0:T(8,128)(2,1)} %bitcast.15, bf16[1,1,1536,768]{3,2,1,0:T(8,128)(2,1)} %w_first.1, ...), custom_call_target="tpu_custom_call" | custom-call | tf_op jit(solution)/shard_map/flow_step/pallas_call | solution.py:507
  190.3 1.9 write_out.1

commit v5 on v4

--- a/solution.py
+++ b/solution.py
@@ -13,6 +13,7 @@
 PAD = 8
 Z_FIRST = 768
 ALONG_Y = 1024
+PAIRS = 4
 
 epsilon = 1e-06
 time_step = 0.25
@@ -75,13 +76,36 @@
 
     left, right = (place + half - 1) % half, (place + 1) % half
 
+    row_x, pair = group // PAIRS, group % PAIRS
+    own_slot = row_x * PAIRS
+
+    def entry(to_group):
+        away = (to_group % PAIRS - pair + PAIRS) % PAIRS
+        odd, far = away % 2, away // 2
+        to_plane = (far + (1 - odd) * plane) % 2
+        slot = own_slot + odd * (1 + plane) + (1 - odd) * far * 3
+        return expert_at(to_group, to_plane * half + place), slot
+
+    def origin(slot):
+        i = slot % PAIRS
+        near, far = ((i + 1) // 2) % 2, i // 3
+        from_pair = (pair + near * (2 * plane - 1) + far * 2 + PAIRS) % PAIRS
+        from_plane = near * (i - 1) + (1 - near) * ((plane + far) % 2)
+        return expert_at((slot // PAIRS) * PAIRS + from_pair, from_plane * half + place)
+
     barrier = pltpu.get_barrier_semaphore()
+
+    def arrive(to):
+        pl.semaphore_signal(barrier, inc=1, device_id=to, device_id_type=MESH)
 
     @pl.loop(1, groups)
     def _(k):
-        pl.semaphore_signal(
-            barrier, inc=1, device_id=expert_at((group + k) % groups, member), device_id_type=MESH
-        )
+        arrive(entry((group + k) % groups)[0])
+        arrive(origin((own_slot + k) % groups))
+
+    @pl.loop(1, samples)
+    def _(k):
+        arrive(expert_at(prompt_half * samples + (sample + k) % samples, member))
 
     @pl.loop(1, members)
     def _(k):
@@ -166,15 +190,27 @@
             device_id=to, device_id_type=MESH,
         ).start()
 
-    def send_across(unit, source, target, send_sem, recv_sem):
-        target[unit, group] = source[unit, group]
+    def send_out(unit):
+        out_recv[unit, own_slot] = out_send[unit, group]
 
         @pl.loop(1, groups)
         def _(k):
             to_group = (group + k) % groups
+            to, slot = entry(to_group)
             send(
-                source.at[unit, to_group], target.at[unit, group], send_sem, recv_sem,
-                expert_at(to_group, member),
+                out_send.at[unit, to_group], out_recv.at[unit, slot],
+                send_sems.at[0, unit], recv_sems.at[0, unit], to,
+            )
+
+    def send_back(unit):
+        home_recv[unit, group] = home_send[unit, own_slot]
+
+        @pl.loop(1, groups)
+        def _(k):
+            slot = (own_slot + k) % groups
+            send(
+                home_send.at[unit, slot], home_recv.at[unit, group],
+                send_sems.at[6, unit], recv_sems.at[12, unit], origin(slot),
             )
 
     def front(layer, micro):
@@ -208,7 +244,7 @@
             return jnp.where(hit, both, 0.0).astype(bf16)
 
         out_send[unit] = pack_rows(normed, spread)
-        send_across(unit, out_send, out_recv, send_sems.at[0, unit], recv_sems.at[0, unit])
+        send_out(unit)
 
     def gather(layer, micro):
         unit = 2 * layer + micro
@@ -339,7 +375,7 @@
         line = line + cross_recv[unit].astype(f32)
         full = jnp.concatenate([total.astype(bf16), line.astype(bf16)], axis=1)
         home_send[unit] = pack_rows(full, lambda part: packing((slots, group_rows), 1, part))
-        send_across(unit, home_send, home_recv, send_sems.at[6, unit], recv_sems.at[12, unit])
+        send_back(unit)
 
     def combine(layer, micro):
         unit = 2 * layer + micro
@@ -362,7 +398,7 @@
         gate = mods[layer, 2, pl.ds(prompt, 1)]
         hid[micro] = (hid[micro].astype(f32) + gate * moe).astype(bf16)
 
-    pl.semaphore_wait(barrier, groups - 1 + members - 1 + keys - 1)
+    pl.semaphore_wait(barrier, 2 * (groups - 1) + samples - 1 + members - 1 + keys - 1)
     for copy in pushes:
         copy.start()
 

time: 192 us -> 190 us (0.990)
  Pallas kernels: 192 us -> 190 us
where the time goes in v5:
time: 190 us
  Pallas kernels  190 us (100%)
    pallas_call x1, Pallas kernels, local(): pl.pallas_call(functools.partial(kernel, sizes), out_shape=(jax.ShapeDtyp...  188 us

profile of v5, /device:TPU:1, one launch (start us, length us, event | category | flops | bytes accessed | tf_op | source)
XLA Modules:
  0.0 190.3 jit_solution(2004134815254823905)
XLA Ops:
  0.6 187.8 %flow_step.1 = (f32[2,16,32]{2,1,0:T(8,128)}, f32[32,16,128]{2,1,0:T(8,128)}) custom-call(f32[4,16,32]{2,1,0:T(8,128)} %bitcast.17, f32[8,1536]{1,0:T(8,128)} %cond.1, f32[16,1536]{1,0:T(8,128)} %w_embed.1, f32[3,8,1536]{2,1,0:T(8,128)} %bitcast.14, bf16[16,1536]{1,0:T(8,128)(2,1)} %bitcast.15, bf16[1,1,1536,768]{3,2,1,0:T(8,128)(2,1)} %w_first.1, ...), custom_call_target="tpu_custom_call" | custom-call | tf_op jit(solution)/shard_map/flow_step/pallas_call | solution.py:543
  188.4 1.9 write_out.1

commit v6 on v5

--- a/solution.py
+++ b/solution.py
@@ -11,7 +11,7 @@
 SEQ = 256
 CAP = 5
 PAD = 8
-Z_FIRST = 768
+Z_FIRST = 512
 ALONG_Y = 1024
 PAIRS = 4
 
@@ -44,7 +44,8 @@
     latents, cond, w_embed, modulation, router_in, w_first, w_second, routes_in, w_final,
     next_out, maps_out,
     hid, mix, routes, mods, router, first, second,
-    out_send, out_recv, rows_in, rows_out, pair_recv, pair_send, own_recv, line_recv, line_send, cross_recv,
+    out_send, out_recv, rows_in, rows_out, pair_recv, pairs, pair_step, pair_turn, line_step, line_turn, line_send,
+    cross_recv,
     home_send, home_recv, stats, stats_recv, maps,
     send_sems, recv_sems, load_sems, push_sems, land_sems, map_sems,
 ):
@@ -74,7 +75,13 @@
         to_half = (to_key // members) % halves
         return {"segment": to_core, "expert": (to_half * samples + sample) * members + to_key % members}
 
-    left, right = (place + half - 1) % half, (place + 1) % half
+    left, right, opposite = (place + half - 1) % half, (place + 1) % half, (place + 2) % half
+
+    def pair_half(side):
+        return pl.ds(side * (cut // 2), cut // 2)
+
+    def line_half(side):
+        return pl.ds(cut + side * ((width - cut) // 2), (width - cut) // 2)
 
     row_x, pair = group // PAIRS, group % PAIRS
     own_slot = row_x * PAIRS
@@ -291,7 +298,7 @@
     def relay_opposite(layer, micro):
         unit = 2 * layer + micro
         wait_bytes(rows_in.at[unit, plane, 0], recv_sems.at[6, unit])
-        cross(unit, (place + 2) % half)
+        cross(unit, opposite)
 
     def expert(unit, layer, of_plane):
         inner = dot(rows_in[unit, of_plane].reshape(half * group_rows, width), first[layer])
@@ -299,13 +306,10 @@
         partial = dot(inner, second[layer]).astype(bf16)
         rows_out[unit, of_plane] = partial.reshape(half, group_rows, width)
 
-        @pl.loop(1, half)
-        def _(k):
-            to_place = (place + k) % half
+        for side in range(2):
             send(
-                rows_out.at[unit, of_plane, to_place, :, pl.ds(cut, width - cut)],
-                line_recv.at[unit, place, of_plane],
-                send_sems.at[3, unit], recv_sems.at[9, unit], in_group(plane, to_place),
+                rows_out.at[unit, of_plane, opposite, :, line_half(side)], line_step.at[unit, side, of_plane],
+                send_sems.at[3, unit], recv_sems.at[9, unit], in_group(plane, (right, left)[side]),
             )
 
     def compute(layer, micro):
@@ -327,37 +331,50 @@
             rows_out.at[unit, far_plane, :, :, pl.ds(0, cut)], pair_recv.at[unit],
             send_sems.at[2, unit], recv_sems.at[7, unit], in_group(far_plane, place),
         )
-        for of_plane in range(2):
-            line_recv[unit, place, of_plane] = rows_out[unit, of_plane, place, :, pl.ds(cut, width - cut)]
+    def turn_line(layer, micro):
+        unit = 2 * layer + micro
+        wait_bytes(line_step.at[unit], recv_sems.at[9, unit])
+        for side, to_place in enumerate((right, left)):
+            for of_plane in range(2):
+                mine = rows_out[unit, of_plane, to_place, :, line_half(side)].astype(f32)
+                rows_out[unit, of_plane, to_place, :, line_half(side)] = (
+                    mine + line_step[unit, side, of_plane].astype(f32)
+                ).astype(bf16)
+            send(
+                rows_out.at[unit, :, to_place, :, pl.ds(cut, width - cut)], line_turn.at[unit, side],
+                send_sems.at[8, unit], recv_sems.at[14, unit], in_group(plane, to_place),
+            )
 
     def reduce_pair(layer, micro):
         unit = 2 * layer + micro
         wait_bytes(pair_recv.at[unit], recv_sems.at[7, unit])
-
-        @pl.loop(0, half)
-        def _(k):
-            to_place = (place + 1 + k) % half
-            mine = rows_out[unit, plane, to_place, :, pl.ds(0, cut)].astype(f32)
-            pair_send[unit, to_place] = (mine + pair_recv[unit, to_place].astype(f32)).astype(bf16)
-
-            @pl.when(k < half - 1)
-            def _():
-                send(
-                    pair_send.at[unit, to_place], own_recv.at[unit, place],
-                    send_sems.at[4, unit], recv_sems.at[10, unit], in_group(plane, to_place),
-                )
-
-        own_recv[unit, place] = pair_send[unit, place]
+        pairs[unit] = (
+            rows_out[unit, plane, :, :, pl.ds(0, cut)].astype(f32) + pair_recv[unit].astype(f32)
+        ).astype(bf16)
+        for side in range(2):
+            send(
+                pairs.at[unit, opposite, :, pair_half(side)], pair_step.at[unit, side],
+                send_sems.at[4, unit], recv_sems.at[10, unit], in_group(plane, (right, left)[side]),
+            )
+
+    def turn_pair(layer, micro):
+        unit = 2 * layer + micro
+        wait_bytes(pair_step.at[unit], recv_sems.at[10, unit])
+        for side, to_place in enumerate((right, left)):
+            mine = pairs[unit, to_place, :, pair_half(side)].astype(f32)
+            pairs[unit, to_place, :, pair_half(side)] = (mine + pair_step[unit, side].astype(f32)).astype(bf16)
+            send(
+                pairs.at[unit, to_place], pair_turn.at[unit, side],
+                send_sems.at[9, unit], recv_sems.at[15, unit], in_group(plane, to_place),
+            )
 
     def line_total(unit, of_plane):
-        total = line_recv[unit, 0, of_plane].astype(f32)
-        for k in range(1, half):
-            total = total + line_recv[unit, k, of_plane].astype(f32)
-        return total
+        mine = rows_out[unit, of_plane, place, :, pl.ds(cut, width - cut)].astype(f32)
+        return mine + line_turn[unit, 0, of_plane].astype(f32) + line_turn[unit, 1, of_plane].astype(f32)
 
     def reduce_line(layer, micro):
         unit = 2 * layer + micro
-        wait_bytes(line_recv.at[unit, pl.ds(0, half - 1)], recv_sems.at[9, unit])
+        wait_bytes(line_turn.at[unit], recv_sems.at[14, unit])
         line_send[unit] = line_total(unit, far_plane).astype(bf16)
         send(
             line_send.at[unit], cross_recv.at[unit],
@@ -366,10 +383,10 @@
 
     def send_home(layer, micro):
         unit = 2 * layer + micro
-        wait_bytes(own_recv.at[unit, pl.ds(0, half - 1)], recv_sems.at[10, unit])
-        total = own_recv[unit, 0].astype(f32)
-        for k in range(1, half):
-            total = total + own_recv[unit, k].astype(f32)
+        wait_bytes(pair_turn.at[unit], recv_sems.at[15, unit])
+        total = pairs[unit, place].astype(f32)
+        for side in range(2):
+            total = total + pair_turn[unit, side].astype(f32)
         line = line_total(unit, plane)
         wait_bytes(cross_recv.at[unit], recv_sems.at[11, unit])
         line = line + cross_recv[unit].astype(f32)
@@ -445,7 +462,12 @@
 
         @pl.loop(0, 2)
         def _(micro):
+            turn_line(layer, micro)
             reduce_pair(layer, micro)
+
+        @pl.loop(0, 2)
+        def _(micro):
+            turn_pair(layer, micro)
             reduce_line(layer, micro)
 
         @pl.loop(0, 2)
@@ -504,8 +526,10 @@
         wait_bytes(rows_in.at[unit, 0], send_sems.at[7, unit])
         wait_bytes(rows_in.at[unit, 0, pl.ds(0, half - 1)], send_sems.at[1, unit])
         wait_bytes(pair_recv.at[unit], send_sems.at[2, unit])
-        wait_bytes(line_recv.at[unit, pl.ds(0, half - 1)], send_sems.at[3, unit])
-        wait_bytes(own_recv.at[unit, pl.ds(0, half - 1)], send_sems.at[4, unit])
+        wait_bytes(line_step.at[unit], send_sems.at[3, unit])
+        wait_bytes(pair_step.at[unit], send_sems.at[4, unit])
+        wait_bytes(line_turn.at[unit], send_sems.at[8, unit])
+        wait_bytes(pair_turn.at[unit], send_sems.at[9, unit])
         wait_bytes(line_send.at[unit], send_sems.at[5, unit])
 
 
@@ -562,8 +586,10 @@
             pltpu.VMEM((4, 2, half, group_rows, width), bf16),
             pltpu.VMEM((4, half, group_rows, Z_FIRST), bf16),
             pltpu.VMEM((4, half, group_rows, Z_FIRST), bf16),
-            pltpu.VMEM((4, half, group_rows, Z_FIRST), bf16),
-            pltpu.VMEM((4, half, 2, group_rows, width - Z_FIRST), bf16),
+            pltpu.VMEM((4, 2, group_rows, Z_FIRST // 2), bf16),
+            pltpu.VMEM((4, 2, group_rows, Z_FIRST), bf16),
+            pltpu.VMEM((4, 2, 2, group_rows, (width - Z_FIRST) // 2), bf16),
+            pltpu.VMEM((4, 2, 2, group_rows, width - Z_FIRST), bf16),
             pltpu.VMEM((4, group_rows, width - Z_FIRST), bf16),
             pltpu.VMEM((4, group_rows, width - Z_FIRST), bf16),
             pltpu.VMEM((4, groups, PAD, block_lanes), bf16),
@@ -571,8 +597,8 @@
             pltpu.VMEM((patch, 4 * rows), f32),
             pltpu.VMEM((SAMPLES, patch, 4 * rows), f32),
             pltpu.VMEM((keys, patch, 4 * rows), f32),
-            pltpu.SemaphoreType.DMA((8, 4)),
-            pltpu.SemaphoreType.DMA((14, 4)),
+            pltpu.SemaphoreType.DMA((10, 4)),
+            pltpu.SemaphoreType.DMA((16, 4)),
             pltpu.SemaphoreType.DMA((5,)),
             pltpu.SemaphoreType.DMA((5,)),
             pltpu.SemaphoreType.DMA((5,)),

time: 190 us -> 189 us (level)
  no operation moved by 1% of the time
where the time goes in v6:
time: 189 us
  Pallas kernels  189 us (100%)
    pallas_call x1, Pallas kernels, local(): pl.pallas_call(functools.partial(kernel, sizes), out_shape=(jax.ShapeDtyp...  187 us

profile of v6, /device:TPU:1, one launch (start us, length us, event | category | flops | bytes accessed | tf_op | source)
XLA Modules:
  0.0 189.3 jit_solution(2656928270986908374)
XLA Ops:
  0.6 186.7 %flow_step.1 = (f32[2,16,32]{2,1,0:T(8,128)}, f32[32,16,128]{2,1,0:T(8,128)}) custom-call(f32[4,16,32]{2,1,0:T(8,128)} %bitcast.17, f32[8,1536]{1,0:T(8,128)} %cond.1, f32[16,1536]{1,0:T(8,128)} %w_embed.1, f32[3,8,1536]{2,1,0:T(8,128)} %bitcast.14, bf16[16,1536]{1,0:T(8,128)(2,1)} %bitcast.15, bf16[1,1,1536,768]{3,2,1,0:T(8,128)(2,1)} %w_first.1, ...), custom_call_target="tpu_custom_call" | custom-call | tf_op jit(solution)/shard_map/flow_step/pallas_call | solution.py:567
  187.4 1.9 %write_out.1 = (f32[2,16,32]{2,1,0:T(8,128)}, f32[8,16,256]{2,1,0:T(8,128)}, f32[8,16,256]{2,1,0:T(8,128)}) custom-call(f32[32,16,128]{2,1,0:T(8,128)} %get-tuple-element.8.maps, f32[2,16,32]{2,1,0:T(8,128)} %get-tuple-element.9.next_in), custom_call_target="tpu_custom_call" | custom-call | tf_op jit(solution)/shard_map/write_out/pallas_call | solution.py:622
